TPU v7x, 256 devices: a whole 4x4x8 slice. The times are simulated.
256 devices in a mesh: grp: 4 (over y), seq: 64 (over z, x, core).
Axes of the slice: x: 4, y: 4, z: 8, core: 2. Of those that a mesh axis runs over, the one named last changes fastest.
Arguments:
- tokens: bfloat16 [1024, 1024], P(('grp', 'seq')), may hold values from -6 to 6
- attn_gain: float32 [1024], replicated, may hold values from 0.1 to 1.9
- w_qkv: bfloat16 [1024, 3072], replicated, may hold values from -0.1875 to 0.1875
- w_out: bfloat16 [1024, 1024], replicated, may hold values from -0.1875 to 0.1875
- mlp_gain: float32 [1024], replicated, may hold values from 0.1 to 1.9
- w_gate_up: bfloat16 [2, 1024, 4096], P(None, None, 'seq'), may hold values from -0.1875 to 0.1875
- w_down: bfloat16 [4096, 1024], P('seq'), may hold values from -0.09375 to 0.09375
- kv_cache: bfloat16 [3072, 2, 64, 1024], P(('grp', 'seq'))
- block_owner: int32 [3072], P(('grp', 'seq')), may hold values from 0 to 255, as said below
- block_fill: int32 [3072], P(('grp', 'seq')), may hold values from 0 to 64, as said below
Outputs:
- output: bfloat16 [1024, 1024], P(('grp', 'seq'))
Inputs may be any that keep to these rules, and one draw needn't show every extreme that they name: `block_fill`: each request has at least one block; in each group one request fills exactly 256 whole blocks, every other has at most 2 blocks; blocks of one request are live from their start and all but its last are full; blocks with no live token exist in every group. `block_owner`: every served request number of a group names some block of that group.
All inputs are finite; a program needn't handle non-finite values.
Results may differ from a plain program's by a relative error of at most 0.024.
Values may be sent and summed in bfloat16 or wider, within the bound.
No kernel may reach another device: no remote copies, remote signals or barrier semaphores. Data moves between devices by JAX's collectives and lax.ppermute only.
A program may use at most 320 MiB of HBM per device.

v0:
```python
import jax
import jax.numpy as jnp
from jax import lax
from jax.sharding import PartitionSpec as P

HEADS = 16


floor_score = -1e30
epsilon = 1e-05


def rms_scaled(row_data, gain):
    values = row_data.astype(jnp.float32)
    return values * lax.rsqrt(jnp.mean(values * values, axis=-1, keepdims=True) + epsilon) * gain


def body(
    tokens, attn_gain, w_qkv, w_out, mlp_gain, w_gate_up, w_down, kv_cache, block_owner, block_fill
):
    groups = lax.axis_size("grp")
    row_count, feature_count = tokens.shape
    head_count = HEADS
    head_dim = feature_count // head_count
    per_group = row_count // groups
    score_scale = head_dim ** (-0.5)
    normed = rms_scaled(tokens, attn_gain).astype(jnp.bfloat16)
    qkv = jnp.dot(normed, w_qkv, preferred_element_type=jnp.float32).astype(jnp.bfloat16)
    sent_qkv, sent_input = (
        lax.all_to_all(
            qkv.reshape(per_group, groups, 3 * feature_count),
            "grp",
            split_axis=1,
            concat_axis=1,
            tiled=True,
        ),
        lax.all_to_all(
            tokens.reshape(per_group, groups, feature_count),
            "grp",
            split_axis=1,
            concat_axis=1,
            tiled=True,
        ),
    )
    served_qkv = sent_qkv.reshape(row_count, 3 * feature_count)
    served_input = sent_input.reshape(row_count, feature_count)
    query_own = served_qkv[:, :feature_count]
    key_own = served_qkv[:, feature_count : 2 * feature_count]
    value_own = served_qkv[:, 2 * feature_count :]
    offset = lax.axis_index("seq") * row_count
    query_all = lax.all_gather(query_own, "seq", axis=0, tiled=True)
    group_rows = query_all.shape[0]
    blocks, _, span, _ = kv_cache.shape
    key_block = kv_cache[:, 0].reshape(blocks, span, head_count, head_dim)
    value_block = kv_cache[:, 1].reshape(blocks, span, head_count, head_dim)
    query_blocks = query_all[block_owner].reshape(blocks, head_count, head_dim)
    scores = (
        jnp.einsum("bhd,bthd->bht", query_blocks, key_block, preferred_element_type=jnp.float32)
        * score_scale
    )
    is_valid = (
        lax.broadcasted_iota(jnp.int32, (blocks, head_count, span), 2) < block_fill[:, None, None]
    )
    masked = jnp.where(is_valid, scores, floor_score)
    block_max = jnp.max(masked, axis=2)
    weights = jnp.where(is_valid, jnp.exp(masked - block_max[:, :, None]), 0.0).astype(jnp.bfloat16)
    block_total = jnp.sum(weights.astype(jnp.float32), axis=2)
    block_sum = jnp.einsum(
        "bht,bthd->bhd", weights, value_block, preferred_element_type=jnp.float32
    )
    member = block_owner[None, :] == lax.broadcasted_iota(jnp.int32, (group_rows, blocks), 0)
    local_max = jnp.max(jnp.where(member[:, :, None], block_max[None, :, :], floor_score), axis=1)
    factor = jnp.exp(block_max - local_max[block_owner])
    member_table = member.astype(jnp.float32)
    local_total = jnp.dot(member_table, block_total * factor, precision=lax.Precision.HIGHEST)
    local_sum = jnp.dot(
        member_table,
        (block_sum * factor[:, :, None]).reshape(blocks, feature_count),
        precision=lax.Precision.HIGHEST,
    )
    own_max = lax.dynamic_slice_in_dim(local_max, offset, row_count, 0)
    own_total = lax.dynamic_slice_in_dim(local_total, offset, row_count, 0)
    own_sum = lax.dynamic_slice_in_dim(local_sum, offset, row_count, 0)
    query_float = query_own.astype(jnp.float32).reshape(row_count, head_count, head_dim)
    key_float = key_own.astype(jnp.float32).reshape(row_count, head_count, head_dim)
    own_score = jnp.sum(query_float * key_float, axis=2) * score_scale
    joined = jnp.maximum(own_max, own_score)
    keep_weight = jnp.exp(own_max - joined)
    own_weight = jnp.exp(own_score - joined)
    new_total = own_total * keep_weight + own_weight
    new_sum = own_sum.reshape(row_count, head_count, head_dim) * keep_weight[:, :, None]
    new_sum = (
        new_sum
        + value_own.astype(jnp.float32).reshape(row_count, head_count, head_dim)
        * own_weight[:, :, None]
    )
    local_max = lax.dynamic_update_slice_in_dim(local_max, joined, offset, 0)
    local_total = lax.dynamic_update_slice_in_dim(local_total, new_total, offset, 0)
    local_sum = lax.dynamic_update_slice_in_dim(
        local_sum, new_sum.reshape(row_count, feature_count), offset, 0
    )
    local_max, local_total, local_sum = (local_max, local_total, local_sum)
    maxima = lax.pmax(local_max, "seq")
    factor = jnp.exp(local_max - maxima)
    scaled_sum = (
        local_sum.reshape(local_sum.shape[0], head_count, head_dim) * factor[:, :, None]
    ).reshape(local_sum.shape)
    totals, weighted = (
        lax.psum_scatter(local_total * factor, "seq", scatter_dimension=0, tiled=True),
        lax.psum_scatter(scaled_sum, "seq", scatter_dimension=0, tiled=True),
    )
    scaled = weighted.reshape(weighted.shape[0], head_count, head_dim) / totals[:, :, None]
    context = scaled.reshape(weighted.shape[0], feature_count).astype(jnp.bfloat16)
    mixed_rows = served_input.astype(jnp.float32) + jnp.dot(
        context, w_out, preferred_element_type=jnp.float32
    )
    normed_mlp = rms_scaled(mixed_rows, mlp_gain).astype(jnp.bfloat16)
    rows_piece = lax.all_gather(normed_mlp, "seq", axis=0, tiled=True)
    gate_part = jnp.dot(rows_piece, w_gate_up[0], preferred_element_type=jnp.float32)
    up_part = jnp.dot(rows_piece, w_gate_up[1], preferred_element_type=jnp.float32)
    hidden = (jax.nn.silu(gate_part) * up_part).astype(jnp.bfloat16)
    partial_value = jnp.dot(hidden, w_down, preferred_element_type=jnp.float32)
    residual, partial_value = (mixed_rows, partial_value)
    down_sum = lax.psum_scatter(partial_value, "seq", scatter_dimension=0, tiled=True)
    output = (residual + down_sum).astype(jnp.bfloat16)
    returned = lax.all_to_all(
        output.reshape(per_group, groups, feature_count),
        "grp",
        split_axis=1,
        concat_axis=1,
        tiled=True,
    )
    return returned.reshape(row_count, feature_count)


def solution(mesh):
    in_specs = (
        P(("grp", "seq"), None),
        P(),
        P(),
        P(),
        P(),
        P(None, None, "seq"),
        P("seq", None),
        P(("grp", "seq"), None, None, None),
        P(("grp", "seq")),
        P(("grp", "seq")),
    )
    out_specs = P(("grp", "seq"), None)
    return jax.shard_map(body, mesh=mesh, in_specs=in_specs, out_specs=out_specs, check_vma=False)
```

profile of v0, /device:TPU:8, one launch (start us, length us, event | category | flops | bytes accessed | tf_op | source)
XLA Modules:
  0.0 859.8 jit_solution(14917239014895460157)
XLA Ops:
  6.5 1.0 fusion.20
  7.5 3.8 fusion
  11.8 0.7 reduce
  12.5 0.6 reshape.124
  13.1 5.4 all-to-all-start.1
  18.6 4.0 fusion.39
  22.6 4.1 copy.67
  26.7 5.3 reshape_squeeze.7
  32.1 52.8 %all-gather = bf16[64,4,1024]{2,1,0:T(4,128)(2,1)S(1)} all-gather(bf16[1,4,1024]{2,1,0:T(4,128)(2,1)S(1)} %slice_bitcast_fusion), channel_id=1, replica_groups=mesh['grp'=4,'seq'=64] {'seq'}, dimensions={0}, use_global_device_ids=true | all-gather | bytes 532480 | tf_op jit(solution)/shard_map/all_gather | solution.py:51
  85.0 0.6 gather_fusion
  85.7 2.8 fusion.40
  90.6 2.8 fusion.1
  93.6 0.7 fusion.26
  94.9 248.7 %pmax.7 = f32[256,16]{0,1:T(8,128)S(1)} all-reduce(f32[256,16]{0,1:T(8,128)S(1)} %dynamic_update_slice.10), channel_id=1, replica_groups=mesh['grp'=4,'seq'=64] {'seq'}, use_global_device_ids=true, to_apply=%region_4.5 | all-reduce | flops 4096 | bytes 32768 | tf_op jit(solution)/shard_map/pmax | solution.py:103
  343.7 0.6 fusion.38
  344.3 1.1 mul.136
  345.3 2.6 copy.56
  348.0 2.4 mul.138
  350.4 0.6 reduce.1
  351.1 0.6 reshape.126
  351.7 4.8 all-to-all-start
  356.5 0.6 dynamic-slice
  357.7 2.6 all-to-all-done
  360.4 246.4 %all-reduce.1 = f32[256,16]{0,1:T(8,128)S(1)} all-reduce(f32[256,16]{0,1:T(8,128)} %get-tuple-element.5), channel_id=3, replica_groups=mesh['grp'=4,'seq'=64] {'seq'}, use_global_device_ids=true, to_apply=%region_7.8.clone | all-reduce | flops 4096 | bytes 32768
  607.1 1.3 multiply_reduce_fusion
  608.4 47.2 %all-gather.1 = bf16[64,4,1024]{2,1,0:T(4,128)(2,1)S(1)} all-gather(bf16[1,4,1024]{2,1,0:T(4,128)(2,1)S(1)} %fusion.28), channel_id=1, replica_groups=mesh['grp'=4,'seq'=64] {'seq'}, dimensions={0}, use_global_device_ids=true | all-gather | bytes 532480 | tf_op jit(solution)/shard_map/all_gather | solution.py:118
  656.1 1.9 fusion.4
  658.0 184.5 %all-reduce.8.cloned.1.call-done = f32[256,1024]{1,0:T(8,128)} async-done(((f32[256,1024]{1,0:T(8,128)}), f32[256,1024]{1,0:T(8,128)}) %all-reduce.8.cloned.1.call-update) | async-done | bytes 1048592
  842.4 0.8 fusion.29
  843.2 0.6 reduce.2
  843.8 8.5 all_to_all.15
  852.3 0.6 copy.84
  (70 shorter events, 4.7 us)
Async XLA Ops:
  6.5 600.5 %copy-start = (bf16[1024,1024]{1,0:T(8,128)(2,1)S(1)}, bf16[1024,1024]{1,0:T(8,128)(2,1)}, u32[]{:S(2)}) copy-start(bf16[1024,1024]{1,0:T(8,128)(2,1)} %param.13) | copy-start | bytes 6291460
  7.5 11.0 %copy-start.6 = (s32[12]{0:T(128)S(1)}, s32[12]{0:T(128)}, u32[]{:S(2)}) copy-start(s32[12]{0:T(128)} %param.18) | copy-start | bytes 148
  13.1 18.9 %all-to-all-start.1 = ((bf16[4,2,1536]{2,1,0:T(2,128)(2,1)}), bf16[4,2,1536]{2,1,0:T(2,128)(2,1)S(1)}, u32[]{:S(2)}, u32[]{:S(2)}) async-start(bf16[4,2,1536]{2,1,0:T(2,128)(2,1)} %reshape.124), calls=%async_computation.1 | async-start | bytes 49152 | tf_op jit(solution)/shard_map/all_to_all | solution.py:30
  18.6 588.5 %all-reduce.6.cloned.1.call-start = ((), (), s32[]{:S(2)}) async-start(), calls=%async_computation.3 | async-start | bytes 2097152
  32.0 56.5 %copy-start.5 = (s32[12]{0:T(128)S(1)}, s32[12]{0:T(128)}, u32[]{:S(2)}) copy-start(s32[12]{0:T(128)} %param.19) | copy-start | bytes 148
  345.3 5.1 copy-start.3
  345.3 11.2 %copy-start.7 = (u32[256]{0:T(256)S(1)}, u32[256]{0:T(256)}, u32[]{:S(2)}) copy-start(u32[256]{0:T(256)} %constant.36) | copy-start | bytes 3076
  350.4 258.0 %copy-start.4 = (f32[1024]{0:T(1024)S(1)}, f32[1024]{0:T(1024)}, u32[]{:S(2)}) copy-start(f32[1024]{0:T(1024)} %param.14) | copy-start | bytes 12292
  350.4 305.4 %copy-start.1 = (bf16[2,1024,64]{1,2,0:T(8,128)(2,1)S(1)}, bf16[2,1024,64]{1,2,0:T(8,128)(2,1)}, u32[]{:S(2)}) copy-start(bf16[2,1024,64]{1,2,0:T(8,128)(2,1)} %param.15) | copy-start | bytes 786436
  350.4 305.7 %copy-start.2 = (bf16[64,1024]{1,0:T(8,128)(2,1)S(1)}, bf16[64,1024]{1,0:T(8,128)(2,1)}, u32[]{:S(2)}) copy-start(bf16[64,1024]{1,0:T(8,128)(2,1)} %param.16) | copy-start | bytes 393220
  351.7 8.7 %all-to-all-start = ((bf16[4,2,512]{2,1,0:T(2,128)(2,1)}), bf16[4,2,512]{2,1,0:T(2,128)(2,1)S(1)}, u32[]{:S(2)}, u32[]{:S(2)}) async-start(bf16[4,2,512]{2,1,0:T(2,128)(2,1)} %reshape.126), calls=%async_computation | async-start | bytes 16384 | tf_op jit(solution)/shard_map/all_to_all | solution.py:37
  356.5 485.9 %all-reduce.8.cloned.1.call-start = ((), (), s32[]{:S(2)}) async-start(), calls=%async_computation.4 | async-start | bytes 2097152
Sparse Core Ops, SparseCore 0:
  350.5 182.9 all-reduce.5
  658.1 184.2 all-reduce.7
where the time goes:
time: 862 us; the launch traced here: 860 us
  blocking collectives  604 us (70%)
  waiting for transfers between devices  187 us (22%)
  local copies, waits for them, and re-layouts  23.3 us (3%)
  between operations  14.3 us (2%)
  matrix products  13.7 us (2%)
  starting transfers between devices  10.2 us (1%)
    pmax x1, blocking collectives, body(): maxima = lax.pmax(local_max, 'seq')  249 us
    unnamed x1, blocking collectives  246 us
    unnamed x4, waiting for transfers between devices  185 us
    all_gather x1, blocking collectives, body(): query_all = lax.all_gather(query_own, 'seq', axis=0, tiled=True)  52.8 us
    all_gather x1, blocking collectives, body(): rows_piece = lax.all_gather(normed_mlp, 'seq', axis=0, tiled=True)  47.2 us
  transfers between devices with their start and end apart: 4, of which 2 were waited for; matrix products, arithmetic and copies ran while one was open for 2% of the time, Pallas kernels for 0%

commit v1 on v0

v1 whole, which is shorter than its diff:
```python
import jax
import jax.numpy as jnp
from jax import lax
from jax.experimental import pallas as pl
from jax.experimental.pallas import tpu as pltpu
from jax.sharding import Mesh, PartitionSpec as P

HEADS = 16
CORES = 2
LANES = 128
FLOOR = -1e30
EPSILON = 1e-05
F32 = jnp.float32
BF16 = jnp.bfloat16


def iota(shape, dim):
    return lax.broadcasted_iota(jnp.int32, shape, dim)


def dot(a, b):
    return jnp.dot(a, b, preferred_element_type=F32)


def pieces(v):
    high = v.astype(BF16)
    return high, (v - high.astype(F32)).astype(BF16)


def head_rows(feature_count, head_dim):
    shape = (LANES, feature_count)
    return (iota(shape, 1) // head_dim == iota(shape, 0)).astype(BF16)


def attend_kernel(owner, fill, got, peer, gain, w_qkv, kv, rows_out, own_out, *, rows, chips, head_dim):
    blocks, _, span, features = kv.shape
    half = got.shape[0]
    count = blocks + rows
    core = lax.axis_index("core")
    chip = lax.axis_index("chip")
    shape = (count, 2 * half)
    line = iota(shape, 0)
    place = jnp.zeros(shape, jnp.int32)
    owner_line = iota((count, LANES), 0)
    owners = jnp.zeros((count, LANES), jnp.int32)
    for b in range(blocks):
        u = owner[b]
        s = u // rows
        at = jnp.where(s % CORES == core, 0, half) + (u % rows) * chips + s // CORES
        place = jnp.where(line == b, at, place)
        owners = jnp.where(owner_line == b, u, owners)
    for i in range(rows):
        place = jnp.where(line == blocks + i, i * chips + chip, place)
        owners = jnp.where(owner_line == blocks + i, (chip * CORES + core) * rows + i, owners)
    select = (place == iota(shape, 1)).astype(BF16)
    inputs = dot(select[:, :half], got[...]) + dot(select[:, half:], peer[...])
    own_out[...] = inputs
    scale = lax.rsqrt(jnp.mean(inputs * inputs, axis=1, keepdims=True) + EPSILON)
    normed = (inputs * scale * gain[...]).astype(BF16)
    qkv = dot(normed, w_qkv[...]).astype(BF16).astype(F32)
    query = qkv[:, :features]
    key_new = qkv[:, features : 2 * features]
    value_new = qkv[:, 2 * features :]

    head_mask = iota((HEADS, features), 1) // head_dim == iota((HEADS, features), 0)
    spread = jnp.concatenate(
        [
            jnp.where(head_mask, jnp.broadcast_to(query[b : b + 1], (HEADS, features)), 0.0)
            for b in range(blocks)
        ],
        axis=0,
    ).astype(BF16)
    keys = kv[:, 0].reshape(blocks * span, features)
    values = kv[:, 1].reshape(blocks * span, features)
    scores = lax.dot_general(
        spread, keys, (((1,), (1,)), ((), ())), preferred_element_type=F32
    ) * (head_dim**-0.5)
    wide = scores.shape
    column = iota(wide, 1)
    column_block = column // span
    limit = jnp.zeros((1, blocks * span), jnp.int32)
    limit_block = iota(limit.shape, 1) // span
    for b in range(blocks):
        limit = jnp.where(limit_block == b, fill[b], limit)
    live = (column_block == iota(wide, 0) // HEADS) & (column - column_block * span < limit)
    masked = jnp.where(live, scores, FLOOR)
    peak = jnp.max(masked, axis=1, keepdims=True)
    weights = jnp.where(live, jnp.exp(masked - peak), 0.0).astype(BF16)
    total = jnp.sum(weights.astype(F32), axis=1, keepdims=True)
    summed = dot(weights, values)
    alive = total > 0.0
    safe = jnp.where(alive, total, 1.0)
    level = jnp.where(alive, peak + jnp.log(safe), FLOOR)
    summed = summed * (1.0 / safe)
    diagonal = iota((HEADS, LANES), 0) == iota((HEADS, LANES), 1)
    for b in range(blocks):
        part = slice(b * HEADS, (b + 1) * HEADS)
        rows_out[b : b + 1, :features] = jnp.sum(
            jnp.where(head_mask, summed[part], 0.0), axis=0, keepdims=True
        )
        rows_out[b : b + 1, features : features + LANES] = jnp.sum(
            jnp.where(diagonal, level[part], 0.0), axis=0, keepdims=True
        )
    shape = (features, LANES)
    by_head = (iota(shape, 0) // head_dim == iota(shape, 1)).astype(BF16)
    high, low = pieces(query * key_new)
    own_score = (dot(high, by_head) + dot(low, by_head)) * (head_dim**-0.5)
    rows_out[blocks:, :features] = value_new[blocks:]
    rows_out[blocks:, features : features + LANES] = own_score[blocks:]
    rows_out[:, features + LANES :] = owners.astype(F32)


def merge_kernel(mine, peer, out, *, rows, head_dim):
    count = 2 * mine.shape[0]
    features = mine.shape[1] - 2 * LANES
    half = out.shape[0]
    core = lax.axis_index("core")
    values = jnp.concatenate([mine[:, :features], peer[:, :features]], axis=0)
    level = jnp.concatenate(
        [mine[:, features : features + LANES], peer[:, features : features + LANES]], axis=0
    )
    owners = jnp.concatenate([mine[:, features + LANES :], peer[:, features + LANES :]], axis=0)
    square = (count, count)
    owner_column = owners[:, :1]
    owner_row = jnp.sum(
        jnp.where(iota(square, 0) == iota(square, 1), owner_column, 0.0), axis=0, keepdims=True
    )
    same = owner_column == owner_row
    peak = jnp.full(level.shape, FLOOR, F32)
    for j in range(count):
        peak = jnp.maximum(
            peak, jnp.where(owners == owners[j : j + 1], level[j : j + 1], FLOOR)
        )
    weight = jnp.exp(level - peak)
    same_table = same.astype(BF16)
    high, low = pieces(weight)
    total = dot(same_table, high) + dot(same_table, low)
    joined = jnp.where(iota(level.shape, 1) < HEADS, peak + jnp.log(total), 0.0)
    heads = head_rows(features, head_dim)
    high, low = pieces(weight / total)
    scaled = values * (dot(high, heads) + dot(low, heads))
    first = (
        jnp.sum(
            jnp.where(same & (iota(square, 0) < iota(square, 1)), 1.0, 0.0), axis=0, keepdims=True
        )
        == 0.0
    )
    owner_row = owner_row.astype(jnp.int32)
    home = owner_row // rows
    place = jnp.where(home % CORES == core, (home // CORES) * rows + owner_row % rows, -1)
    chosen = iota((half, count), 0) == place
    table = chosen.astype(BF16)
    high, low = pieces(scaled)
    out[:, :features] = (dot(table, high) + dot(table, low)).astype(BF16)
    one = joined.astype(BF16)
    rest = joined - one.astype(F32)
    two = rest.astype(BF16)
    three = (rest - two.astype(F32)).astype(BF16)
    packed = (
        one.astype(F32)
        + pltpu.roll(two.astype(F32), HEADS, 1)
        + pltpu.roll(three.astype(F32), 2 * HEADS, 1)
    ).astype(BF16)
    first_table = (chosen & first).astype(BF16)
    stats = dot(first_table, packed)
    absent = jnp.sum(table.astype(F32), axis=1, keepdims=True) == 0.0
    out[:, features:] = jnp.where(
        absent & (iota(stats.shape, 1) < HEADS), FLOOR, stats
    ).astype(BF16)


def project_kernel(got, inputs, w_out, gain, mixed_out, sent, *, rows, head_dim):
    half = got.shape[0]
    features = w_out.shape[0]
    sub = 8
    parts = half // sub
    stats = got[:, features:].astype(F32)
    level = stats + pltpu.roll(stats, LANES - HEADS, 1) + pltpu.roll(stats, LANES - 2 * HEADS, 1)
    level = jnp.where(iota(level.shape, 1) < HEADS, level, FLOOR)
    level = level.reshape(parts, sub, LANES)
    peak = jnp.max(level, axis=0)
    peak = jnp.maximum(peak, pltpu.roll(peak, rows, 0))
    weight = jnp.exp(level - peak[None])
    total = jnp.sum(weight, axis=0)
    total = total + pltpu.roll(total, rows, 0)
    weight = (weight / total[None]).reshape(half, LANES)
    heads = head_rows(features, head_dim)
    high, low = pieces(weight)
    spread = dot(high, heads) + dot(low, heads)
    scaled = got[:, :features].astype(F32) * spread
    weighted = jnp.sum(scaled.reshape(parts, sub, features), axis=0)
    context = (weighted + pltpu.roll(weighted, rows, 0)).astype(BF16)
    last = inputs[inputs.shape[0] - sub :, :]
    last = jnp.where(iota(last.shape, 0) < rows, pltpu.roll(last, rows, 0), last)
    mixed = last + dot(context, w_out[...])
    mixed_out[...] = mixed
    scale = lax.rsqrt(jnp.mean(mixed * mixed, axis=1, keepdims=True) + EPSILON)
    normed = mixed * scale * gain[...]
    sent[...] = jnp.concatenate([normed] * parts, axis=0).astype(BF16)


def hidden_kernel(got, peer, w_gate_up, w_down, mixed, own_out, sent, *, rows, chips):
    half = got.shape[0]
    chip = lax.axis_index("chip")
    shape = (half, half)
    line = iota(shape, 0)
    order = (iota(shape, 1) == (line % chips) * rows + line // chips).astype(BF16)

    def down(part):
        gate = dot(part, w_gate_up[0])
        up = dot(part, w_gate_up[1])
        hidden = (gate / (1.0 + jnp.exp(-gate)) * up).astype(BF16)
        return dot(dot(order, hidden).astype(BF16), w_down[...])

    sent[...] = down(peer[...]).astype(BF16)
    own_out[...] = down(got[...])
    for i in range(rows):
        at = pl.ds(i * chips + chip, 1)
        own_out[at, :] = own_out[at, :] + mixed[i : i + 1, :]


def call(kernel, out_shape, smem=0, args=(), limit=48 << 20):
    vmem = pl.BlockSpec(memory_space=pltpu.VMEM)
    scalar = pl.BlockSpec(memory_space=pltpu.SMEM)
    specs = [scalar] * smem + [vmem] * (len(args) - smem)
    return pl.pallas_call(
        kernel,
        out_shape=out_shape,
        in_specs=specs,
        out_specs=jax.tree.map(lambda _: vmem, out_shape),
        compiler_params=pltpu.CompilerParams(vmem_limit_bytes=limit),
    )(*args)


def body(
    tokens, attn_gain, w_qkv, w_out, mlp_gain, w_gate_up, w_down, kv_cache, block_owner, block_fill
):
    groups = lax.axis_size("grp")
    chips = lax.axis_size("chip")
    rows, features = tokens.shape
    head_dim = features // HEADS
    blocks = kv_cache.shape[0]
    half = rows * chips
    count = blocks + rows
    swap = [(0, 1), (1, 0)]
    every = ("grp", "chip")

    def shape(dims, kind):
        return jax.ShapeDtypeStruct(dims, kind)

    sent = jnp.broadcast_to(tokens[:, None, :], (groups, chips, features))
    got = lax.all_to_all(sent.reshape(groups * chips, features), every, 0, 0, tiled=True)
    peer = lax.ppermute(got, "core", swap)
    partial, inputs = call(
        lambda *refs: attend_kernel(*refs, rows=rows, chips=chips, head_dim=head_dim),
        (shape((count, features + 2 * LANES), F32), shape((count, features), F32)),
        smem=2,
        args=(block_owner, block_fill, got, peer, attn_gain.reshape(1, features), w_qkv, kv_cache),
    )
    partial_peer = lax.ppermute(partial, "core", swap)
    sent = call(
        lambda *refs: merge_kernel(*refs, rows=rows, head_dim=head_dim),
        shape((half, features + LANES), BF16),
        args=(partial, partial_peer),
    )
    got = lax.all_to_all(sent, "chip", 0, 0, tiled=True)
    mixed, sent = call(
        lambda *refs: project_kernel(*refs, rows=rows, head_dim=head_dim),
        (shape((8, features), F32), shape((half, features), BF16)),
        args=(got, inputs, w_out, mlp_gain.reshape(1, features)),
    )
    got = lax.all_to_all(sent, "chip", 0, 0, tiled=True)
    peer = lax.ppermute(got, "core", swap)
    own, sent = call(
        lambda *refs: hidden_kernel(*refs, rows=rows, chips=chips),
        (shape((half, features), F32), shape((half, features), BF16)),
        args=(got, peer, w_gate_up, w_down, mixed),
    )
    peer = lax.ppermute(sent, "core", swap)
    sent = (own + peer.astype(F32)).astype(BF16)
    got = lax.all_to_all(sent, every, 0, 0, tiled=True)
    output = jnp.sum(got.reshape(groups, chips, features).astype(F32), axis=1)
    return output.astype(BF16)


def solution(mesh):
    groups, shards = mesh.devices.shape
    devices = mesh.devices.reshape(groups, shards // CORES, CORES)
    fine = Mesh(devices, ("grp", "chip", "core"))
    seq = ("chip", "core")
    whole = ("grp", "chip", "core")
    in_specs = (
        P(whole, None),
        P(),
        P(),
        P(),
        P(),
        P(None, None, seq),
        P(seq, None),
        P(whole, None, None, None),
        P(whole),
        P(whole),
    )
    return jax.shard_map(
        body, mesh=fine, in_specs=in_specs, out_specs=P(whole, None), check_vma=False
    )
```

time: 862 us -> 108 us (0.13)
  blocking collectives: 604 us -> 83.4 us
  waiting for transfers between devices: 187 us -> 5.3 us
  local copies, waits for them, and re-layouts: 23.3 us -> 6.37 us
  between operations: 14.3 us -> 0.2 us
  matrix products: 13.7 us -> 0 us
  starting transfers between devices: 10.2 us -> 0.62 us
    pmax x1 -> x0, blocking collectives: 249 us -> none  [body(): maxima = lax.pmax(local_max, 'seq')]
    unnamed x1 -> x0, blocking collectives: 246 us -> none
    unnamed x4 -> x0, waiting for transfers between devices: 185 us -> none
    all_gather x2 -> x0, blocking collectives: 100 us -> none  [the longest x1 52.8 us: body(): query_all = lax.all_gather(query_own, 'seq', axis=0, tiled=True)]
    all_to_all x1 -> x4, blocking collectives: 8.48 us -> 83.4 us  [the longest x2 34 us: body(): got = lax.all_to_all(sent, 'chip', 0, 0, tiled=True)]
    dot_general x8 -> x0, matrix products: 13.7 us -> none  [the longest x1 3.79 us: body(): jnp.dot(normed, w_qkv, preferred_element_type=jnp.float32)]
    all_to_all x2 -> x0, starting transfers between devices: 10.2 us -> none  [the longest x1 5.41 us: body(): lax.all_to_all(qkv.reshape(per_group, groups, 3 * feature_count), 'grp',...]
    another operation x2 -> x0, local copies, waits for them, and re-layouts: 9.37 us -> none  [the longest x1 5.25 us: body(): value_block = kv_cache[:, 1].reshape(blocks, span, head_count, head_dim)]
  transfers between devices with their start and end apart: 4 -> 4, of which waited for: 2 -> 4; matrix products, arithmetic and copies ran while one was open for 2% -> 0% of each run, Pallas kernels for 0% -> 0%
where the time goes in v1:
time: 108 us; the launch traced here: 107 us
  blocking collectives  83.4 us (77%)
  Pallas kernels  8.04 us (7%)
  local copies, waits for them, and re-layouts  6.37 us (6%)
  waiting for transfers between devices  5.3 us (5%)
  other arithmetic  2.96 us (3%)
    all_to_all x2, blocking collectives, body(): got = lax.all_to_all(sent, 'chip', 0, 0, tiled=True)  34 us
    all_to_all x1, blocking collectives, body(): lax.all_to_all(sent.reshape(groups * chips, features), every, 0, 0, tiled...  28.9 us
    all_to_all x1, blocking collectives, body(): got = lax.all_to_all(sent, every, 0, 0, tiled=True)  20.5 us
    pallas_call x4, Pallas kernels, call(): pl.pallas_call(kernel, out_shape=out_shape, in_specs=specs, out_specs=jax...  8.04 us
    unnamed x23, local copies, waits for them, and re-layouts  4.67 us
    ppermute x2, waiting for transfers between devices, body(): peer = lax.ppermute(got, 'core', swap)  2.75 us
  transfers between devices with their start and end apart: 4, of which 4 were waited for; matrix products, arithmetic and copies ran while one was open for 0% of the time, Pallas kernels for 0%

profile of v1, /device:TPU:8, one launch (start us, length us, event | category | flops | bytes accessed | tf_op | source)
XLA Modules:
  0.0 106.9 jit_solution(17154546330619596116)
XLA Ops:
  0.0 0.9 broadcast_in_dim.2
  0.9 0.5 broadcast.1
  1.4 1.5 %reduce.1 = bf16[128,1024]{1,0:T(8,128)(2,1)} reduce(bf16[128,1,1024]{2,0,1:T(8,128)(2,1)S(1)} %bitcast.14, bf16[]{:T(256)} %broadcast.1), dimensions={1}, to_apply=%copy.14.reduce_sub_computation | reduce | bytes 524290 | tf_op jit(solution)/shard_map/all_to_all | solution.py:252
  2.9 1.8 %reshape.24 = bf16[128,2,512]{2,1,0:T(2,128)(2,1)} reshape(bf16[128,1024]{1,0:T(8,128)(2,1)} %reduce.1) | data formatting | bytes 524288
  4.7 28.9 %all_to_all.42 = bf16[128,2,512]{2,1,0:T(2,128)(2,1)S(1)} all-to-all(bf16[128,2,512]{2,1,0:T(2,128)(2,1)} %reshape.24), channel_id=1, replica_groups=mesh['grp'=4,'chip'=32,'core'=2] {'grp','chip'}, dimensions={0} | all-to-all | bytes 524288 | tf_op jit(solution)/shard_map/all_to_all | solution.py:252
  33.6 0.9 reshape.25
  34.5 1.1 %copy.20 = bf16[128,1,1024]{2,0,1:T(8,128)(2,1)S(1)} copy(bf16[128,1,1024]{2,1,0:T(2,128)(2,1)} %reshape.25) | data formatting | bytes 524288
  35.7 0.1 collective-permute-start
  35.8 1.5 %collective-permute-done.refs_3_ = bf16[128,1024]{1,0:T(8,128)(2,1)S(1)} collective-permute-done((bf16[128,1024]{1,0:T(8,128)(2,1)S(1)}, bf16[128,1024]{1,0:T(8,128)(2,1)S(1)}, u32[]{:S(2)}, u32[]{:S(2)}) %collective-permute-start) | collective-permute-done | bytes 262176 | tf_op jit(solution)/shard_map/ppermute | solution.py:253
  37.3 5.5 %shard_map.100 = (f32[16,1280]{1,0:T(8,128)S(1)}, f32[16,1024]{1,0:T(8,128)S(1)}) custom-call(s32[12]{0:T(128)S(1)} %copy-done.5, s32[12]{0:T(128)S(1)} %copy-done.6, bf16[128,1024]{1,0:T(8,128)(2,1)S(1)} %bitcast.10, bf16[128,1024]{1,0:T(8,128)(2,1)S(1)} %collective-permute-done.refs_3_, f32[1,1024]{1,0:T(1,128)S(1)} %bitcast.11, ...), custom_call_target="tpu_custom_call" | custom-call | tf_op jit(solution)/shard_map/pallas_call | solution.py:226
  42.8 0.2 collective-permute-start.1
  43.0 1.1 %collective-permute-done.1.refs_1_ = f32[16,1280]{1,0:T(8,128)S(1)} collective-permute-done((f32[16,1280]{1,0:T(8,128)S(1)}, f32[16,1280]{1,0:T(8,128)S(1)}, u32[]{:S(2)}, u32[]{:S(2)}) %collective-permute-start.1) | collective-permute-done | bytes 81952 | tf_op jit(solution)/shard_map/ppermute | solution.py:260
  44.2 0.7 shard_map.101
  44.9 0.1 all_to_all.30
  44.9 18.1 %all_to_all.43 = bf16[32,4,1152]{2,1,0:T(4,128)(2,1)S(1)} all-to-all(bf16[32,4,1152]{2,1,0:T(4,128)(2,1)S(1)} %all_to_all.30), channel_id=1, replica_groups=mesh['grp'=4,'chip'=32,'core'=2] {'chip'}, dimensions={0} | all-to-all | bytes 589824 | tf_op jit(solution)/shard_map/all_to_all | solution.py:266
  63.0 0.1 all_to_all.32.refs_0_
  63.1 0.8 shard_map.102
  63.9 0.1 all_to_all.33
  64.0 16.0 %all_to_all.44 = bf16[32,4,1024]{2,1,0:T(4,128)(2,1)S(1)} all-to-all(bf16[32,4,1024]{2,1,0:T(4,128)(2,1)S(1)} %all_to_all.33), channel_id=1, replica_groups=mesh['grp'=4,'chip'=32,'core'=2] {'chip'}, dimensions={0} | all-to-all | bytes 524288 | tf_op jit(solution)/shard_map/all_to_all | solution.py:272
  80.0 0.1 all_to_all.35.refs_0_
  80.1 0.1 collective-permute-start.2
  80.2 0.3 copy.15.refs_2_
  80.5 1.2 %collective-permute-done.2.refs_1_ = bf16[128,1024]{1,0:T(8,128)(2,1)S(1)} collective-permute-done((bf16[128,1024]{1,0:T(8,128)(2,1)S(1)}, bf16[128,1024]{1,0:T(8,128)(2,1)S(1)}, u32[]{:S(2)}, u32[]{:S(2)}) %collective-permute-start.2) | collective-permute-done | bytes 262176 | tf_op jit(solution)/shard_map/ppermute | solution.py:273
  81.7 1.1 %shard_map.103 = (f32[128,1024]{1,0:T(8,128)S(1)}, bf16[128,1024]{1,0:T(8,128)(2,1)S(1)}) custom-call(bf16[128,1024]{1,0:T(8,128)(2,1)S(1)} %all_to_all.35.refs_0_, bf16[128,1024]{1,0:T(8,128)(2,1)S(1)} %collective-permute-done.2.refs_1_, bf16[2,1024,64]{2,1,0:T(8,128)(2,1)S(1)} %copy.15.refs_2_, bf16[64,1024]{1,0:T(8,128)(2,1)S(1)} %copy-done.2, ...), custom_call_target="tpu_custom_call" | custom-call | tf_op jit(solution)/shard_map/pallas_call | solution.py:226
  82.8 0.2 collective-permute-start.3
  83.0 1.4 %collective-permute-done.3 = bf16[128,1024]{1,0:T(8,128)(2,1)S(1)} collective-permute-done((bf16[128,1024]{1,0:T(8,128)(2,1)S(1)}, bf16[128,1024]{1,0:T(8,128)(2,1)S(1)}, u32[]{:S(2)}, u32[]{:S(2)}) %collective-permute-start.3) | collective-permute-done | bytes 262176 | tf_op jit(solution)/shard_map/ppermute | solution.py:279
  84.5 0.8 reduce.2
  85.3 0.2 reshape.26
  85.5 20.5 %all_to_all.45 = bf16[128,2,512]{2,1,0:T(2,128)(2,1)S(1)} all-to-all(bf16[128,2,512]{2,1,0:T(2,128)(2,1)S(1)} %reshape.26), channel_id=1, replica_groups=mesh['grp'=4,'chip'=32,'core'=2] {'grp','chip'}, dimensions={0} | all-to-all | bytes 524288 | tf_op jit(solution)/shard_map/all_to_all | solution.py:281
  105.9 0.2 reshape.27
  106.2 0.1 copy.18
  106.3 0.7 reduce_sum.12
  (17 shorter events, 0.1 us)
Async XLA Ops:
  0.0 37.3 %copy-start.6 = (s32[12]{0:T(128)S(1)}, s32[12]{0:T(128)}, u32[]{:S(2)}) copy-start(s32[12]{0:T(128)} %refs_1_.1) | copy-start | bytes 148
  0.0 37.3 %copy-start.5 = (s32[12]{0:T(128)S(1)}, s32[12]{0:T(128)}, u32[]{:S(2)}) copy-start(s32[12]{0:T(128)} %refs_0_.1) | copy-start | bytes 148
  0.0 37.3 %copy-start = (bf16[12,2,64,1024]{3,2,1,0:T(8,128)(2,1)S(1)}, bf16[12,2,64,1024]{3,2,1,0:T(8,128)(2,1)}, u32[]{:S(2)}) copy-start(bf16[12,2,64,1024]{3,2,1,0:T(8,128)(2,1)} %refs_6_.1) | copy-start | bytes 9437188
  0.0 37.3 %copy-start.3 = (f32[1024]{0:T(1024)S(1)}, f32[1024]{0:T(1024)}, u32[]{:S(2)}) copy-start(f32[1024]{0:T(1024)} %param.11) | copy-start | bytes 12292
  35.7 1.6 %collective-permute-start = (bf16[128,1024]{1,0:T(8,128)(2,1)S(1)}, bf16[128,1024]{1,0:T(8,128)(2,1)S(1)}, u32[]{:S(2)}, u32[]{:S(2)}) collective-permute-start(bf16[128,1024]{1,0:T(8,128)(2,1)S(1)} %bitcast.9), channel_id=1, source_target_pairs={{0,1},{1,0},{2,3},{3,2},{4,5},{5,4},{6,7},{7,6},{8,9},{9,8},{10,11... | collective-permute-start | bytes 786440 | tf_op jit(solution)/shard_map/ppermute | solution.py:253
  37.3 25.8 %copy-start.4 = (f32[1024]{0:T(1024)S(1)}, f32[1024]{0:T(1024)}, u32[]{:S(2)}) copy-start(f32[1024]{0:T(1024)} %param.14) | copy-start | bytes 12292
  42.8 20.3 %copy-start.1 = (bf16[1024,1024]{1,0:T(8,128)(2,1)S(1)}, bf16[1024,1024]{1,0:T(8,128)(2,1)}, u32[]{:S(2)}) copy-start(bf16[1024,1024]{1,0:T(8,128)(2,1)} %refs_2_.2) | copy-start | bytes 6291460
  42.8 37.4 %copy-start.7 = (bf16[2,1024,64]{1,2,0:T(8,128)(2,1)S(1)}, bf16[2,1024,64]{1,2,0:T(8,128)(2,1)}, u32[]{:S(2)}) copy-start(bf16[2,1024,64]{1,2,0:T(8,128)(2,1)} %param.15) | copy-start | bytes 786436
  42.8 1.4 %collective-permute-start.1 = (f32[16,1280]{1,0:T(8,128)S(1)}, f32[16,1280]{1,0:T(8,128)S(1)}, u32[]{:S(2)}, u32[]{:S(2)}) collective-permute-start(f32[16,1280]{1,0:T(8,128)S(1)} %get-tuple-element.11.refs_0_), channel_id=1, source_target_pairs={{0,1},{1,0},{2,3},{3,2},{4,5},{5,4},{6,7},{7,6},{8,9},{9,8},{10,11... | collective-permute-start | bytes 245768 | tf_op jit(solution)/shard_map/ppermute | solution.py:260
  44.9 36.8 %copy-start.2 = (bf16[64,1024]{1,0:T(8,128)(2,1)S(1)}, bf16[64,1024]{1,0:T(8,128)(2,1)}, u32[]{:S(2)}) copy-start(bf16[64,1024]{1,0:T(8,128)(2,1)} %refs_3_.1) | copy-start | bytes 393220
  80.1 1.6 %collective-permute-start.2 = (bf16[128,1024]{1,0:T(8,128)(2,1)S(1)}, bf16[128,1024]{1,0:T(8,128)(2,1)S(1)}, u32[]{:S(2)}, u32[]{:S(2)}) collective-permute-start(bf16[128,1024]{1,0:T(8,128)(2,1)S(1)} %all_to_all.35.refs_0_), channel_id=1, source_target_pairs={{0,1},{1,0},{2,3},{3,2},{4,5},{5,4},{6,7},{7,6},{8,9},{9,8},{10,11... | collective-permute-start | bytes 786440 | tf_op jit(solution)/shard_map/ppermute | solution.py:273
  82.8 1.6 %collective-permute-start.3 = (bf16[128,1024]{1,0:T(8,128)(2,1)S(1)}, bf16[128,1024]{1,0:T(8,128)(2,1)S(1)}, u32[]{:S(2)}, u32[]{:S(2)}) collective-permute-start(bf16[128,1024]{1,0:T(8,128)(2,1)S(1)} %get-tuple-element.16), channel_id=1, source_target_pairs={{0,1},{1,0},{2,3},{3,2},{4,5},{5,4},{6,7},{7,6},{8,9},{9,8},{10,11... | collective-permute-start | bytes 786440 | tf_op jit(solution)/shard_map/ppermute | solution.py:279

commit v2 on v1

--- a/solution.py
+++ b/solution.py
@@ -8,6 +8,7 @@
 HEADS = 16
 CORES = 2
 LANES = 128
+SUB = 8
 FLOOR = -1e30
 EPSILON = 1e-05
 F32 = jnp.float32
@@ -32,35 +33,71 @@
     return (iota(shape, 1) // head_dim == iota(shape, 0)).astype(BF16)
 
 
-def attend_kernel(owner, fill, got, peer, gain, w_qkv, kv, rows_out, own_out, *, rows, chips, head_dim):
-    blocks, _, span, features = kv.shape
-    half = got.shape[0]
-    count = blocks + rows
+def lay_flat(tiles):
+    return jnp.concatenate([tiles[:, j, :] for j in range(SUB)], axis=1)
+
+
+def spread_kernel(tokens, out, tiles, *, chips):
+    rows, features = tokens.shape
+    width = features // SUB
+    values = tokens[...].astype(F32)
+    for j in range(SUB):
+        tiles[:, j, :] = values[:, j * width : (j + 1) * width]
+    for g in range(rows):
+        row = tiles[g].astype(BF16)
+        out[g * chips : (g + 1) * chips] = jnp.broadcast_to(row[None], (chips,) + row.shape)
+
+
+def finish_kernel(got, out, tiles, *, chips):
+    rows, features = out.shape
+    width = features // SUB
+    for g in range(rows):
+        tiles[g] = jnp.sum(got[g * chips : (g + 1) * chips].astype(F32), axis=0)
+    out[...] = lay_flat(tiles).astype(BF16)
+
+
+def rms_scaled(values, gain):
+    scale = lax.rsqrt(jnp.mean(values * values, axis=1, keepdims=True) + EPSILON)
+    return (values * scale * gain).astype(BF16)
+
+
+def own_kernel(got, gain, w_qkv, rows_out, own_out, tiles, *, rows, chips, head_dim):
     core = lax.axis_index("core")
     chip = lax.axis_index("chip")
-    shape = (count, 2 * half)
-    line = iota(shape, 0)
-    place = jnp.zeros(shape, jnp.int32)
-    owner_line = iota((count, LANES), 0)
-    owners = jnp.zeros((count, LANES), jnp.int32)
+    for k in range(SUB):
+        tiles[k] = got[(k % rows) * chips + chip].astype(F32)
+    inputs = lay_flat(tiles)
+    own_out[...] = inputs
+    features = inputs.shape[1]
+    qkv = dot(rms_scaled(inputs, gain[...]), w_qkv[...]).astype(BF16).astype(F32)
+    query = qkv[:, :features]
+    key_new = qkv[:, features : 2 * features]
+    shape = (features, LANES)
+    by_head = (iota(shape, 0) // head_dim == iota(shape, 1)).astype(BF16)
+    high, low = pieces(query * key_new)
+    rows_out[:, :features] = qkv[:, 2 * features :]
+    rows_out[:, features : features + LANES] = (dot(high, by_head) + dot(low, by_head)) * (
+        head_dim**-0.5
+    )
+    owners = (chip * CORES + core) * rows + iota((SUB, LANES), 0) % rows
+    rows_out[:, features + LANES :] = owners.astype(F32)
+
+
+def attend_kernel(
+    owner, fill, got, peer, own, gain, w_qkv, kv, rows_out, tiles, *, rows, chips, head_dim
+):
+    blocks, _, span, features = kv.shape
+    core = lax.axis_index("core")
+    owner_line = iota((blocks, LANES), 0)
+    owners = jnp.zeros((blocks, LANES), jnp.int32)
     for b in range(blocks):
         u = owner[b]
         s = u // rows
-        at = jnp.where(s % CORES == core, 0, half) + (u % rows) * chips + s // CORES
-        place = jnp.where(line == b, at, place)
+        at = (u % rows) * chips + s // CORES
+        tiles[b] = jnp.where(s % CORES == core, got[at].astype(F32), peer[at].astype(F32))
         owners = jnp.where(owner_line == b, u, owners)
-    for i in range(rows):
-        place = jnp.where(line == blocks + i, i * chips + chip, place)
-        owners = jnp.where(owner_line == blocks + i, (chip * CORES + core) * rows + i, owners)
-    select = (place == iota(shape, 1)).astype(BF16)
-    inputs = dot(select[:, :half], got[...]) + dot(select[:, half:], peer[...])
-    own_out[...] = inputs
-    scale = lax.rsqrt(jnp.mean(inputs * inputs, axis=1, keepdims=True) + EPSILON)
-    normed = (inputs * scale * gain[...]).astype(BF16)
-    qkv = dot(normed, w_qkv[...]).astype(BF16).astype(F32)
-    query = qkv[:, :features]
-    key_new = qkv[:, features : 2 * features]
-    value_new = qkv[:, 2 * features :]
+    inputs = lay_flat(tiles)
+    query = dot(rms_scaled(inputs, gain[...]), w_qkv[:, :features]).astype(BF16).astype(F32)
 
     head_mask = iota((HEADS, features), 1) // head_dim == iota((HEADS, features), 0)
     spread = jnp.concatenate(
@@ -101,13 +138,8 @@
         rows_out[b : b + 1, features : features + LANES] = jnp.sum(
             jnp.where(diagonal, level[part], 0.0), axis=0, keepdims=True
         )
-    shape = (features, LANES)
-    by_head = (iota(shape, 0) // head_dim == iota(shape, 1)).astype(BF16)
-    high, low = pieces(query * key_new)
-    own_score = (dot(high, by_head) + dot(low, by_head)) * (head_dim**-0.5)
-    rows_out[blocks:, :features] = value_new[blocks:]
-    rows_out[blocks:, features : features + LANES] = own_score[blocks:]
-    rows_out[:, features + LANES :] = owners.astype(F32)
+    rows_out[:blocks, features + LANES :] = owners.astype(F32)
+    rows_out[blocks:, :] = own[SUB - rows :, :]
 
 
 def merge_kernel(mine, peer, out, *, rows, head_dim):
@@ -172,7 +204,7 @@
 def project_kernel(got, inputs, w_out, gain, mixed_out, sent, *, rows, head_dim):
     half = got.shape[0]
     features = w_out.shape[0]
-    sub = 8
+    sub = SUB
     parts = half // sub
     stats = got[:, features:].astype(F32)
     level = stats + pltpu.roll(stats, LANES - HEADS, 1) + pltpu.roll(stats, LANES - 2 * HEADS, 1)
@@ -190,36 +222,41 @@
     scaled = got[:, :features].astype(F32) * spread
     weighted = jnp.sum(scaled.reshape(parts, sub, features), axis=0)
     context = (weighted + pltpu.roll(weighted, rows, 0)).astype(BF16)
-    last = inputs[inputs.shape[0] - sub :, :]
-    last = jnp.where(iota(last.shape, 0) < rows, pltpu.roll(last, rows, 0), last)
-    mixed = last + dot(context, w_out[...])
-    mixed_out[...] = mixed
-    scale = lax.rsqrt(jnp.mean(mixed * mixed, axis=1, keepdims=True) + EPSILON)
-    normed = mixed * scale * gain[...]
-    sent[...] = jnp.concatenate([normed] * parts, axis=0).astype(BF16)
-
-
-def hidden_kernel(got, peer, w_gate_up, w_down, mixed, own_out, sent, *, rows, chips):
-    half = got.shape[0]
+    mixed = inputs[...] + dot(context, w_out[...])
+    width = features // SUB
+    for j in range(SUB):
+        mixed_out[:, j, :] = mixed[:, j * width : (j + 1) * width]
+    sent[...] = jnp.concatenate([rms_scaled(mixed, gain[...]).astype(F32)] * parts, axis=0).astype(BF16)
+
+
+def down_tiles(part, w_gate_up, w_down, tiles, *, rows, chips):
+    half = part.shape[0]
+    nt = (((1,), (1,)), ((), ()))
+    gate = lax.dot_general(part[...], w_gate_up[0], nt, preferred_element_type=F32)
+    up = lax.dot_general(part[...], w_gate_up[1], nt, preferred_element_type=F32)
+    hidden = (gate / (1.0 + jnp.exp(-gate)) * up).astype(BF16)
+    line = iota((half, half), 0)
+    order = (iota((half, half), 1) == (line % chips) * rows + line // chips).astype(BF16)
+    result = dot(dot(order, hidden).astype(BF16), w_down[...])
+    width = result.shape[1] // SUB
+    for j in range(SUB):
+        tiles[:, j, :] = result[:, j * width : (j + 1) * width]
+
+
+def peer_hidden_kernel(part, w_gate_up, w_down, out, tiles, *, rows, chips):
+    down_tiles(part, w_gate_up, w_down, tiles, rows=rows, chips=chips)
+    out[...] = tiles[...].astype(BF16)
+
+
+def own_hidden_kernel(part, w_gate_up, w_down, mixed, out, *, rows, chips):
+    down_tiles(part, w_gate_up, w_down, out, rows=rows, chips=chips)
     chip = lax.axis_index("chip")
-    shape = (half, half)
-    line = iota(shape, 0)
-    order = (iota(shape, 1) == (line % chips) * rows + line // chips).astype(BF16)
-
-    def down(part):
-        gate = dot(part, w_gate_up[0])
-        up = dot(part, w_gate_up[1])
-        hidden = (gate / (1.0 + jnp.exp(-gate)) * up).astype(BF16)
-        return dot(dot(order, hidden).astype(BF16), w_down[...])
-
-    sent[...] = down(peer[...]).astype(BF16)
-    own_out[...] = down(got[...])
     for i in range(rows):
-        at = pl.ds(i * chips + chip, 1)
-        own_out[at, :] = own_out[at, :] + mixed[i : i + 1, :]
-
-
-def call(kernel, out_shape, smem=0, args=(), limit=48 << 20):
+        at = i * chips + chip
+        out[at] = out[at] + mixed[i]
+
+
+def call(kernel, out_shape, args, smem=0, scratch=(), limit=24 << 20, cost=None):
     vmem = pl.BlockSpec(memory_space=pltpu.VMEM)
     scalar = pl.BlockSpec(memory_space=pltpu.SMEM)
     specs = [scalar] * smem + [vmem] * (len(args) - smem)
@@ -228,7 +265,9 @@
         out_shape=out_shape,
         in_specs=specs,
         out_specs=jax.tree.map(lambda _: vmem, out_shape),
+        scratch_shapes=[pltpu.VMEM(dims, F32) for dims in scratch],
         compiler_params=pltpu.CompilerParams(vmem_limit_bytes=limit),
+        cost_estimate=cost,
     )(*args)
 
 
@@ -242,45 +281,73 @@
     blocks = kv_cache.shape[0]
     half = rows * chips
     count = blocks + rows
+    width = features // SUB
     swap = [(0, 1), (1, 0)]
     every = ("grp", "chip")
-
-    def shape(dims, kind):
+    sizes = dict(rows=rows, chips=chips)
+
+    def shape(kind, *dims):
         return jax.ShapeDtypeStruct(dims, kind)
 
-    sent = jnp.broadcast_to(tokens[:, None, :], (groups, chips, features))
-    got = lax.all_to_all(sent.reshape(groups * chips, features), every, 0, 0, tiled=True)
+    sent = call(
+        lambda *refs: spread_kernel(*refs, chips=chips),
+        shape(BF16, groups * chips, SUB, width),
+        (tokens,),
+        scratch=[(rows, SUB, width)],
+        cost=pl.CostEstimate(flops=10**11, transcendentals=0, bytes_accessed=1 << 18),
+    )
+    got = lax.all_to_all(sent, every, 0, 0, tiled=True)
     peer = lax.ppermute(got, "core", swap)
-    partial, inputs = call(
-        lambda *refs: attend_kernel(*refs, rows=rows, chips=chips, head_dim=head_dim),
-        (shape((count, features + 2 * LANES), F32), shape((count, features), F32)),
+    gain = attn_gain.reshape(1, features)
+    own, inputs = call(
+        lambda *refs: own_kernel(*refs, head_dim=head_dim, **sizes),
+        (shape(F32, SUB, features + 2 * LANES), shape(F32, SUB, features)),
+        (got, gain, w_qkv),
+        scratch=[(SUB, SUB, width)],
+        cost=pl.CostEstimate(flops=1, transcendentals=0, bytes_accessed=1),
+    )
+    partial = call(
+        lambda *refs: attend_kernel(*refs, head_dim=head_dim, **sizes),
+        shape(F32, count, features + 2 * LANES),
+        (block_owner, block_fill, got, peer, own, gain, w_qkv, kv_cache),
         smem=2,
-        args=(block_owner, block_fill, got, peer, attn_gain.reshape(1, features), w_qkv, kv_cache),
+        scratch=[(blocks, SUB, width)],
     )
     partial_peer = lax.ppermute(partial, "core", swap)
     sent = call(
         lambda *refs: merge_kernel(*refs, rows=rows, head_dim=head_dim),
-        shape((half, features + LANES), BF16),
-        args=(partial, partial_peer),
+        shape(BF16, half, features + LANES),
+        (partial, partial_peer),
     )
     got = lax.all_to_all(sent, "chip", 0, 0, tiled=True)
     mixed, sent = call(
         lambda *refs: project_kernel(*refs, rows=rows, head_dim=head_dim),
-        (shape((8, features), F32), shape((half, features), BF16)),
-        args=(got, inputs, w_out, mlp_gain.reshape(1, features)),
+        (shape(F32, SUB, SUB, width), shape(BF16, half, features)),
+        (got, inputs, w_out, mlp_gain.reshape(1, features)),
     )
     got = lax.all_to_all(sent, "chip", 0, 0, tiled=True)
     peer = lax.ppermute(got, "core", swap)
-    own, sent = call(
-        lambda *refs: hidden_kernel(*refs, rows=rows, chips=chips),
-        (shape((half, features), F32), shape((half, features), BF16)),
-        args=(got, peer, w_gate_up, w_down, mixed),
+    w_wide = jnp.swapaxes(w_gate_up, 1, 2)
+    sent = call(
+        lambda *refs: peer_hidden_kernel(*refs, **sizes),
+        shape(BF16, half, SUB, width),
+        (peer, w_wide, w_down),
+        scratch=[(half, SUB, width)],
     )
     peer = lax.ppermute(sent, "core", swap)
+    own = call(
+        lambda *refs: own_hidden_kernel(*refs, **sizes),
+        shape(F32, half, SUB, width),
+        (got, w_wide, w_down, mixed),
+    )
     sent = (own + peer.astype(F32)).astype(BF16)
     got = lax.all_to_all(sent, every, 0, 0, tiled=True)
-    output = jnp.sum(got.reshape(groups, chips, features).astype(F32), axis=1)
-    return output.astype(BF16)
+    return call(
+        lambda *refs: finish_kernel(*refs, chips=chips),
+        shape(BF16, rows, features),
+        (got,),
+        scratch=[(rows, SUB, width)],
+    )
 
 
 def solution(mesh):

time: 108 us -> 97.7 us (0.905)
  local copies, waits for them, and re-layouts: 6.37 us -> 1.44 us
  other arithmetic: 2.96 us -> 0.05 us
  waiting for transfers between devices: 5.3 us -> 3.39 us
    all_to_all x1 -> x2, blocking collectives: 20.5 us -> 49.5 us  [body(): got = lax.all_to_all(sent, every, 0, 0, tiled=True)]
    all_to_all x1 -> x0, blocking collectives: 28.9 us -> none  [body(): lax.all_to_all(sent.reshape(groups * chips, features), every, 0, 0, tiled...]
    unnamed x23 -> x20, local copies, waits for them, and re-layouts: 4.67 us -> 1.12 us
    all_to_all x3 -> x0, other arithmetic: 2.29 us -> none  [the longest x1 1.45 us: body(): lax.all_to_all(sent.reshape(groups * chips, features), every, 0, 0, tiled...]
    pallas_call x4 -> x8, Pallas kernels: 8.04 us -> 7.47 us  [call(): pl.pallas_call(kernel, out_shape=out_shape, in_specs=specs, out_specs=jax...]
  transfers between devices with their start and end apart: 4 -> 4, of which waited for: 4 -> 4; matrix products, arithmetic and copies ran while one was open for 0% -> 0% of each run, Pallas kernels for 0% -> 2%
where the time goes in v2:
time: 97.7 us; the launch traced here: 97 us
  blocking collectives  83.6 us (86%)
  Pallas kernels  7.47 us (8%)
  waiting for transfers between devices  3.39 us (3%)
  local copies, waits for them, and re-layouts  1.44 us (1%)
    all_to_all x2, blocking collectives, body(): got = lax.all_to_all(sent, every, 0, 0, tiled=True)  49.5 us
    all_to_all x2, blocking collectives, body(): got = lax.all_to_all(sent, 'chip', 0, 0, tiled=True)  34.1 us
    pallas_call x8, Pallas kernels, call(): pl.pallas_call(kernel, out_shape=out_shape, in_specs=specs, out_specs=jax...  7.47 us
  transfers between devices with their start and end apart: 4, of which 4 were waited for; matrix products, arithmetic and copies ran while one was open for 0% of the time, Pallas kernels for 2%

profile of v2, /device:TPU:8, one launch (start us, length us, event | category | flops | bytes accessed | tf_op | source)
XLA Modules:
  0.0 97.0 jit_solution(17514573049240419866)
XLA Ops:
  0.0 0.7 copy-done.9
  0.8 29.0 %all_to_all.32.refs_0_.refs_2_ = bf16[128,8,128]{2,1,0:T(8,128)(2,1)S(1)} all-to-all(bf16[128,8,128]{2,1,0:T(8,128)(2,1)S(1)} %shard_map.100), channel_id=1, replica_groups=mesh['grp'=4,'chip'=32,'core'=2] {'grp','chip'}, dimensions={0} | all-to-all | bytes 524288 | tf_op jit(solution)/shard_map/all_to_all | solution.py:299
  29.8 0.0 collective-permute-start
  29.8 0.0 copy-start.1
  29.8 0.0 copy-start.7
  29.8 0.0 copy-start.8
  29.8 1.1 %shard_map.101 = (f32[8,1280]{1,0:T(8,128)S(1)}, f32[8,1024]{1,0:T(8,128)S(1)}) custom-call(bf16[128,8,128]{2,1,0:T(8,128)(2,1)S(1)} %all_to_all.32.refs_0_.refs_2_, f32[1,1024]{1,0:T(1,128)S(1)} %bitcast.5, bf16[1024,3072]{1,0:T(8,128)(2,1)S(1)} %copy-done), custom_call_target="tpu_custom_call" | custom-call | flops 1 | bytes 1 | tf_op jit(solution)/shard_map/pallas_call | solution.py:263
  30.9 0.4 collective-permute-done.refs_3_
  31.3 0.4 copy-done.1
  31.7 2.5 %shard_map.102.refs_0_ = f32[16,1280]{1,0:T(8,128)S(1)} custom-call(s32[12]{0:T(128)S(1)} %copy-done.7, s32[12]{0:T(128)S(1)} %copy-done.8, bf16[128,8,128]{2,1,0:T(8,128)(2,1)S(1)} %all_to_all.32.refs_0_.refs_2_, bf16[128,8,128]{2,1,0:T(8,128)(2,1)S(1)} %collective-permute-done.refs_3_, f32[8,1280]{1,0:T(8,128)S(1)} %get-tuple-element.9.refs_4_, ...), custom_call_target="tpu_custom_call" | custom-call | tf_op jit(solution)/shard_map/pallas_call | solution.py:263
  34.1 0.0 copy-start.2
  34.2 0.0 copy-start.3
  34.2 0.0 copy-start.4
  34.2 0.6 collective-permute-start.1
  34.8 0.9 collective-permute-done.1.refs_1_
  35.7 0.7 shard_map.103
  36.4 0.1 all_to_all.21
  36.5 18.2 %all_to_all.33 = bf16[32,4,1152]{2,1,0:T(4,128)(2,1)S(1)} all-to-all(bf16[32,4,1152]{2,1,0:T(4,128)(2,1)S(1)} %all_to_all.21), channel_id=1, replica_groups=mesh['grp'=4,'chip'=32,'core'=2] {'chip'}, dimensions={0} | all-to-all | bytes 589824 | tf_op jit(solution)/shard_map/all_to_all | solution.py:322
  54.6 0.1 all_to_all.23.refs_0_
  54.7 0.8 shard_map.104
  55.5 0.1 all_to_all.24
  55.7 16.0 %all_to_all.34 = bf16[32,4,1024]{2,1,0:T(4,128)(2,1)S(1)} all-to-all(bf16[32,4,1024]{2,1,0:T(4,128)(2,1)S(1)} %all_to_all.24), channel_id=1, replica_groups=mesh['grp'=4,'chip'=32,'core'=2] {'chip'}, dimensions={0} | all-to-all | bytes 524288 | tf_op jit(solution)/shard_map/all_to_all | solution.py:328
  71.6 0.1 all_to_all.26.refs_0_
  71.7 0.1 collective-permute-start.2
  71.8 1.5 %collective-permute-done.2.refs_0_ = bf16[128,1024]{1,0:T(8,128)(2,1)S(1)} collective-permute-done((bf16[128,1024]{1,0:T(8,128)(2,1)S(1)}, bf16[128,1024]{1,0:T(8,128)(2,1)S(1)}, u32[]{:S(2)}, u32[]{:S(2)}) %collective-permute-start.2) | collective-permute-done | bytes 262176 | tf_op jit(solution)/shard_map/ppermute | solution.py:329
  73.3 0.9 shard_map.106
  74.2 0.2 collective-permute-start.3
  74.4 0.8 shard_map.105
  75.2 0.6 collective-permute-done.3
  75.8 0.1 add_convert_fusion
  75.9 20.5 %all_to_all.35.refs_0_ = bf16[128,8,128]{2,1,0:T(8,128)(2,1)S(1)} all-to-all(bf16[128,8,128]{2,1,0:T(8,128)(2,1)S(1)} %add_convert_fusion), channel_id=1, replica_groups=mesh['grp'=4,'chip'=32,'core'=2] {'grp','chip'}, dimensions={0} | all-to-all | bytes 524288 | tf_op jit(solution)/shard_map/all_to_all | solution.py:344
  96.4 0.7 shard_map.107
  (13 shorter events, 0.1 us)
Async XLA Ops:
  0.0 29.8 %copy-start.5 = (f32[1024]{0:T(1024)S(1)}, f32[1024]{0:T(1024)}, u32[]{:S(2)}) copy-start(f32[1024]{0:T(1024)} %param.11) | copy-start | bytes 12292
  0.0 0.7 copy-start.9
  0.7 29.0 %copy-start = (bf16[1024,3072]{1,0:T(8,128)(2,1)S(1)}, bf16[1024,3072]{1,0:T(8,128)(2,1)}, u32[]{:S(2)}) copy-start(bf16[1024,3072]{1,0:T(8,128)(2,1)} %refs_6_.1) | copy-start | bytes 18874372
  29.8 1.5 %collective-permute-start = (bf16[128,8,128]{2,1,0:T(8,128)(2,1)S(1)}, bf16[128,8,128]{2,1,0:T(8,128)(2,1)S(1)}, u32[]{:S(2)}, u32[]{:S(2)}) collective-permute-start(bf16[128,8,128]{2,1,0:T(8,128)(2,1)S(1)} %all_to_all.32.refs_0_.refs_2_), channel_id=1, source_target_pairs={{0,1},{1,0},{2,3},{3,2},{4,5},{5,4},{6,7},{7,6},{8,9},{9,8},{10,11... | collective-permute-start | bytes 786440 | tf_op jit(solution)/shard_map/ppermute | solution.py:300
  29.8 1.9 %copy-start.1 = (bf16[12,2,64,1024]{3,2,1,0:T(8,128)(2,1)S(1)}, bf16[12,2,64,1024]{3,2,1,0:T(8,128)(2,1)}, u32[]{:S(2)}) copy-start(bf16[12,2,64,1024]{3,2,1,0:T(8,128)(2,1)} %refs_7_.1) | copy-start | bytes 9437188
  29.8 1.9 %copy-start.7 = (s32[12]{0:T(128)S(1)}, s32[12]{0:T(128)}, u32[]{:S(2)}) copy-start(s32[12]{0:T(128)} %refs_0_.3) | copy-start | bytes 148
  29.8 1.9 %copy-start.8 = (s32[12]{0:T(128)S(1)}, s32[12]{0:T(128)}, u32[]{:S(2)}) copy-start(s32[12]{0:T(128)} %refs_1_.1) | copy-start | bytes 148
  31.7 23.0 %copy-start.6 = (f32[1024]{0:T(1024)S(1)}, f32[1024]{0:T(1024)}, u32[]{:S(2)}) copy-start(f32[1024]{0:T(1024)} %param.14) | copy-start | bytes 12292
  34.1 20.6 %copy-start.2 = (bf16[1024,1024]{1,0:T(8,128)(2,1)S(1)}, bf16[1024,1024]{1,0:T(8,128)(2,1)}, u32[]{:S(2)}) copy-start(bf16[1024,1024]{1,0:T(8,128)(2,1)} %refs_2_.5) | copy-start | bytes 6291460
  34.2 39.2 %copy-start.3 = (bf16[2,1024,64]{1,2,0:T(8,128)(2,1)S(1)}, bf16[2,1024,64]{1,2,0:T(8,128)(2,1)}, u32[]{:S(2)}) copy-start(bf16[2,1024,64]{1,2,0:T(8,128)(2,1)} %param.15) | copy-start | bytes 786436
  34.2 39.1 %copy-start.4 = (bf16[64,1024]{1,0:T(8,128)(2,1)S(1)}, bf16[64,1024]{1,0:T(8,128)(2,1)}, u32[]{:S(2)}) copy-start(bf16[64,1024]{1,0:T(8,128)(2,1)} %refs_2_.7) | copy-start | bytes 393220
  34.2 1.5 %collective-permute-start.1 = (f32[16,1280]{1,0:T(8,128)S(1)}, f32[16,1280]{1,0:T(8,128)S(1)}, u32[]{:S(2)}, u32[]{:S(2)}) collective-permute-start(f32[16,1280]{1,0:T(8,128)S(1)} %shard_map.102.refs_0_), channel_id=1, source_target_pairs={{0,1},{1,0},{2,3},{3,2},{4,5},{5,4},{6,7},{7,6},{8,9},{9,8},{10,11... | collective-permute-start | bytes 245768 | tf_op jit(solution)/shard_map/ppermute | solution.py:316
  71.7 1.6 %collective-permute-start.2 = (bf16[128,1024]{1,0:T(8,128)(2,1)S(1)}, bf16[128,1024]{1,0:T(8,128)(2,1)S(1)}, u32[]{:S(2)}, u32[]{:S(2)}) collective-permute-start(bf16[128,1024]{1,0:T(8,128)(2,1)S(1)} %all_to_all.26.refs_0_), channel_id=1, source_target_pairs={{0,1},{1,0},{2,3},{3,2},{4,5},{5,4},{6,7},{7,6},{8,9},{9,8},{10,11... | collective-permute-start | bytes 786440 | tf_op jit(solution)/shard_map/ppermute | solution.py:329
  74.2 1.6 %collective-permute-start.3 = (bf16[128,8,128]{2,1,0:T(8,128)(2,1)S(1)}, bf16[128,8,128]{2,1,0:T(8,128)(2,1)S(1)}, u32[]{:S(2)}, u32[]{:S(2)}) collective-permute-start(bf16[128,8,128]{2,1,0:T(8,128)(2,1)S(1)} %shard_map.106), channel_id=1, source_target_pairs={{0,1},{1,0},{2,3},{3,2},{4,5},{5,4},{6,7},{7,6},{8,9},{9,8},{10,11... | collective-permute-start | bytes 786440 | tf_op jit(solution)/shard_map/ppermute | solution.py:337

commit v3 on v2

--- a/solution.py
+++ b/solution.py
@@ -7,10 +7,12 @@
 
 HEADS = 16
 CORES = 2
+X_CHIPS = 4
 LANES = 128
 SUB = 8
 FLOOR = -1e30
 EPSILON = 1e-05
+CHIP = ("z", "x")
 F32 = jnp.float32
 BF16 = jnp.bfloat16
 
@@ -37,22 +39,35 @@
     return jnp.concatenate([tiles[:, j, :] for j in range(SUB)], axis=1)
 
 
-def spread_kernel(tokens, out, tiles, *, chips):
+def spread_kernel(tokens, w_gate_up, w_down, out, packed, held, tiles, sems, *, chips):
     rows, features = tokens.shape
     width = features // SUB
-    values = tokens[...].astype(F32)
+    units = w_down.shape[0]
+    copies = [
+        pltpu.make_async_copy(w_gate_up.at[0], packed.at[pl.ds(0, units)], sems.at[0]),
+        pltpu.make_async_copy(w_gate_up.at[1], packed.at[pl.ds(units, units)], sems.at[1]),
+        pltpu.make_async_copy(w_down, packed.at[pl.ds(2 * units, units)], sems.at[2]),
+    ]
+    first = pltpu.make_async_copy(tokens, held, sems.at[3])
+    first.start()
+    for copy in copies:
+        copy.start()
+    first.wait()
+    values = held[...].astype(F32)
     for j in range(SUB):
         tiles[:, j, :] = values[:, j * width : (j + 1) * width]
     for g in range(rows):
         row = tiles[g].astype(BF16)
         out[g * chips : (g + 1) * chips] = jnp.broadcast_to(row[None], (chips,) + row.shape)
-
-
-def finish_kernel(got, out, tiles, *, chips):
-    rows, features = out.shape
-    width = features // SUB
+    for copy in copies:
+        copy.wait()
+
+
+def finish_kernel(got, out, tiles):
+    rows = out.shape[0]
+    sources = got.shape[0] // rows
     for g in range(rows):
-        tiles[g] = jnp.sum(got[g * chips : (g + 1) * chips].astype(F32), axis=0)
+        tiles[g] = jnp.sum(got[g * sources : (g + 1) * sources].astype(F32), axis=0)
     out[...] = lay_flat(tiles).astype(BF16)
 
 
@@ -63,7 +78,7 @@
 
 def own_kernel(got, gain, w_qkv, rows_out, own_out, tiles, *, rows, chips, head_dim):
     core = lax.axis_index("core")
-    chip = lax.axis_index("chip")
+    chip = lax.axis_index(CHIP)
     for k in range(SUB):
         tiles[k] = got[(k % rows) * chips + chip].astype(F32)
     inputs = lay_flat(tiles)
@@ -142,10 +157,10 @@
     rows_out[blocks:, :] = own[SUB - rows :, :]
 
 
-def merge_kernel(mine, peer, out, *, rows, head_dim):
+def merge_kernel(mine, peer, out, flat, *, rows, head_dim):
     count = 2 * mine.shape[0]
     features = mine.shape[1] - 2 * LANES
-    half = out.shape[0]
+    half = flat.shape[0]
     core = lax.axis_index("core")
     values = jnp.concatenate([mine[:, :features], peer[:, :features]], axis=0)
     level = jnp.concatenate(
@@ -183,7 +198,7 @@
     chosen = iota((half, count), 0) == place
     table = chosen.astype(BF16)
     high, low = pieces(scaled)
-    out[:, :features] = (dot(table, high) + dot(table, low)).astype(BF16)
+    flat[:, :features] = dot(table, high) + dot(table, low)
     one = joined.astype(BF16)
     rest = joined - one.astype(F32)
     two = rest.astype(BF16)
@@ -196,17 +211,19 @@
     first_table = (chosen & first).astype(BF16)
     stats = dot(first_table, packed)
     absent = jnp.sum(table.astype(F32), axis=1, keepdims=True) == 0.0
-    out[:, features:] = jnp.where(
-        absent & (iota(stats.shape, 1) < HEADS), FLOOR, stats
-    ).astype(BF16)
-
-
-def project_kernel(got, inputs, w_out, gain, mixed_out, sent, *, rows, head_dim):
+    flat[:, features:] = jnp.where(absent & (iota(stats.shape, 1) < HEADS), FLOOR, stats)
+    for n in range(out.shape[0]):
+        out[n] = flat[n * rows : (n + 1) * rows, :].astype(BF16)
+
+
+def project_kernel(parts_in, inputs, w_out, gain, mixed_out, sent, got, *, rows, head_dim):
     half = got.shape[0]
+    for n in range(parts_in.shape[0]):
+        got[n * rows : (n + 1) * rows, :] = parts_in[n].astype(F32)
     features = w_out.shape[0]
     sub = SUB
     parts = half // sub
-    stats = got[:, features:].astype(F32)
+    stats = got[:, features:]
     level = stats + pltpu.roll(stats, LANES - HEADS, 1) + pltpu.roll(stats, LANES - 2 * HEADS, 1)
     level = jnp.where(iota(level.shape, 1) < HEADS, level, FLOOR)
     level = level.reshape(parts, sub, LANES)
@@ -219,53 +236,68 @@
     heads = head_rows(features, head_dim)
     high, low = pieces(weight)
     spread = dot(high, heads) + dot(low, heads)
-    scaled = got[:, :features].astype(F32) * spread
+    scaled = got[:, :features] * spread
     weighted = jnp.sum(scaled.reshape(parts, sub, features), axis=0)
     context = (weighted + pltpu.roll(weighted, rows, 0)).astype(BF16)
     mixed = inputs[...] + dot(context, w_out[...])
     width = features // SUB
     for j in range(SUB):
         mixed_out[:, j, :] = mixed[:, j * width : (j + 1) * width]
-    sent[...] = jnp.concatenate([rms_scaled(mixed, gain[...]).astype(F32)] * parts, axis=0).astype(BF16)
-
-
-def down_tiles(part, w_gate_up, w_down, tiles, *, rows, chips):
-    half = part.shape[0]
-    nt = (((1,), (1,)), ((), ()))
-    gate = lax.dot_general(part[...], w_gate_up[0], nt, preferred_element_type=F32)
-    up = lax.dot_general(part[...], w_gate_up[1], nt, preferred_element_type=F32)
-    hidden = (gate / (1.0 + jnp.exp(-gate)) * up).astype(BF16)
-    line = iota((half, half), 0)
-    order = (iota((half, half), 1) == (line % chips) * rows + line // chips).astype(BF16)
-    result = dot(dot(order, hidden).astype(BF16), w_down[...])
+    normed = rms_scaled(mixed, gain[...]).astype(F32)
+    sent[...] = jnp.concatenate([normed] * (sent.shape[0] // sub), axis=0).astype(BF16)
+
+
+def hidden_kernel(part, mixed, *refs, rows):
+    *weights, out, held, held_down, tiles, sems = refs
+    units = weights[0].shape[0] // 3
+    total = held_down.shape[0]
+    first, last = [], []
+    for n, weight in enumerate(weights):
+        for k in range(2):
+            target = held.at[pl.ds(k * total + n * units, units)]
+            first.append(pltpu.make_async_copy(weight.at[pl.ds(k * units, units)], target, sems.at[3 * n + k]))
+        target = held_down.at[pl.ds(n * units, units)]
+        last.append(pltpu.make_async_copy(weight.at[pl.ds(2 * units, units)], target, sems.at[3 * n + 2]))
+    for copy in first + last:
+        copy.start()
+    count = part.shape[0]
+    line = iota((count, count), 0)
+    per = count // rows
+    order = (iota((count, count), 1) == (line % per) * rows + line // per).astype(BF16)
+    inputs = dot(order, part[...]).astype(BF16)
+    for copy in first:
+        copy.wait()
+    both = lax.dot_general(
+        inputs, held[...], (((1,), (1,)), ((), ())), preferred_element_type=F32
+    )
+    gate = both[:, :total]
+    hidden = (gate / (1.0 + jnp.exp(-gate)) * both[:, total:]).astype(BF16)
+    for copy in last:
+        copy.wait()
+    result = dot(hidden, held_down[...])
     width = result.shape[1] // SUB
     for j in range(SUB):
         tiles[:, j, :] = result[:, j * width : (j + 1) * width]
-
-
-def peer_hidden_kernel(part, w_gate_up, w_down, out, tiles, *, rows, chips):
-    down_tiles(part, w_gate_up, w_down, tiles, rows=rows, chips=chips)
+    z = lax.axis_index("z")
+    for i in range(rows):
+        tiles[i * per + z] = tiles[i * per + z] + mixed[i]
     out[...] = tiles[...].astype(BF16)
 
 
-def own_hidden_kernel(part, w_gate_up, w_down, mixed, out, *, rows, chips):
-    down_tiles(part, w_gate_up, w_down, out, rows=rows, chips=chips)
-    chip = lax.axis_index("chip")
-    for i in range(rows):
-        at = i * chips + chip
-        out[at] = out[at] + mixed[i]
-
-
-def call(kernel, out_shape, args, smem=0, scratch=(), limit=24 << 20, cost=None):
+def call(kernel, out_shape, args, smem=0, hbm=(), out_specs=None, scratch=(), limit=12 << 20, cost=None):
     vmem = pl.BlockSpec(memory_space=pltpu.VMEM)
     scalar = pl.BlockSpec(memory_space=pltpu.SMEM)
     specs = [scalar] * smem + [vmem] * (len(args) - smem)
+    args = list(args)
+    for i in hbm:
+        specs[i] = pl.BlockSpec(memory_space=pltpu.HBM)
+        args[i] = pltpu.with_memory_space_constraint(args[i], pltpu.HBM)
     return pl.pallas_call(
         kernel,
         out_shape=out_shape,
         in_specs=specs,
-        out_specs=jax.tree.map(lambda _: vmem, out_shape),
-        scratch_shapes=[pltpu.VMEM(dims, F32) for dims in scratch],
+        out_specs=jax.tree.map(lambda _: vmem, out_shape) if out_specs is None else out_specs,
+        scratch_shapes=scratch,
         compiler_params=pltpu.CompilerParams(vmem_limit_bytes=limit),
         cost_estimate=cost,
     )(*args)
@@ -275,35 +307,47 @@
     tokens, attn_gain, w_qkv, w_out, mlp_gain, w_gate_up, w_down, kv_cache, block_owner, block_fill
 ):
     groups = lax.axis_size("grp")
-    chips = lax.axis_size("chip")
+    z_chips = lax.axis_size("z")
+    x_chips = lax.axis_size("x")
+    chips = z_chips * x_chips
     rows, features = tokens.shape
     head_dim = features // HEADS
     blocks = kv_cache.shape[0]
+    units = w_down.shape[0]
     half = rows * chips
     count = blocks + rows
     width = features // SUB
     swap = [(0, 1), (1, 0)]
-    every = ("grp", "chip")
+    every = ("grp",) + CHIP
     sizes = dict(rows=rows, chips=chips)
 
     def shape(kind, *dims):
         return jax.ShapeDtypeStruct(dims, kind)
 
-    sent = call(
+    def tiles(n):
+        return pltpu.VMEM((n, SUB, width), F32)
+
+    sent, packed = call(
         lambda *refs: spread_kernel(*refs, chips=chips),
-        shape(BF16, groups * chips, SUB, width),
-        (tokens,),
-        scratch=[(rows, SUB, width)],
+        (shape(BF16, groups * chips, SUB, width), shape(BF16, 3 * units, features)),
+        (tokens, jnp.swapaxes(w_gate_up, 1, 2), w_down),
+        hbm=(0, 1, 2),
+        scratch=[pltpu.VMEM((rows, features), BF16), tiles(rows), pltpu.SemaphoreType.DMA((4,))],
         cost=pl.CostEstimate(flops=10**11, transcendentals=0, bytes_accessed=1 << 18),
     )
+    weights = [packed] + [
+        lax.ppermute(packed, "x", [(i, (i + k) % x_chips) for i in range(x_chips)])
+        for k in range(1, x_chips)
+    ]
     got = lax.all_to_all(sent, every, 0, 0, tiled=True)
     peer = lax.ppermute(got, "core", swap)
+    weights = weights + [lax.ppermute(weight, "core", swap) for weight in weights]
     gain = attn_gain.reshape(1, features)
     own, inputs = call(
         lambda *refs: own_kernel(*refs, head_dim=head_dim, **sizes),
         (shape(F32, SUB, features + 2 * LANES), shape(F32, SUB, features)),
         (got, gain, w_qkv),
-        scratch=[(SUB, SUB, width)],
+        scratch=[tiles(SUB)],
         cost=pl.CostEstimate(flops=1, transcendentals=0, bytes_accessed=1),
     )
     partial = call(
@@ -311,51 +355,50 @@
         shape(F32, count, features + 2 * LANES),
         (block_owner, block_fill, got, peer, own, gain, w_qkv, kv_cache),
         smem=2,
-        scratch=[(blocks, SUB, width)],
+        scratch=[tiles(blocks)],
     )
     partial_peer = lax.ppermute(partial, "core", swap)
     sent = call(
         lambda *refs: merge_kernel(*refs, rows=rows, head_dim=head_dim),
-        shape(BF16, half, features + LANES),
+        shape(BF16, chips, rows, features + LANES),
         (partial, partial_peer),
-    )
-    got = lax.all_to_all(sent, "chip", 0, 0, tiled=True)
+        scratch=[pltpu.VMEM((half, features + LANES), F32)],
+    )
+    got = lax.all_to_all(sent, CHIP, 0, 0, tiled=True)
     mixed, sent = call(
         lambda *refs: project_kernel(*refs, rows=rows, head_dim=head_dim),
-        (shape(F32, SUB, SUB, width), shape(BF16, half, features)),
+        (shape(F32, SUB, SUB, width), shape(BF16, rows * z_chips, features)),
         (got, inputs, w_out, mlp_gain.reshape(1, features)),
-    )
-    got = lax.all_to_all(sent, "chip", 0, 0, tiled=True)
-    peer = lax.ppermute(got, "core", swap)
-    w_wide = jnp.swapaxes(w_gate_up, 1, 2)
+        scratch=[pltpu.VMEM((half, features + LANES), F32)],
+    )
+    got = lax.all_to_all(sent, "z", 0, 0, tiled=True)
     sent = call(
-        lambda *refs: peer_hidden_kernel(*refs, **sizes),
-        shape(BF16, half, SUB, width),
-        (peer, w_wide, w_down),
-        scratch=[(half, SUB, width)],
-    )
-    peer = lax.ppermute(sent, "core", swap)
-    own = call(
-        lambda *refs: own_hidden_kernel(*refs, **sizes),
-        shape(F32, half, SUB, width),
-        (got, w_wide, w_down, mixed),
-    )
-    sent = (own + peer.astype(F32)).astype(BF16)
-    got = lax.all_to_all(sent, every, 0, 0, tiled=True)
+        lambda *refs: hidden_kernel(*refs, rows=rows),
+        shape(BF16, rows * z_chips, SUB, width),
+        [got, mixed] + weights,
+        hbm=range(2, 2 + len(weights)),
+        scratch=[
+            pltpu.VMEM((2 * len(weights) * units, features), BF16),
+            pltpu.VMEM((len(weights) * units, features), BF16),
+            tiles(rows * z_chips),
+            pltpu.SemaphoreType.DMA((3 * len(weights),)),
+        ],
+    )
+    got = lax.all_to_all(sent, ("grp", "z"), 0, 0, tiled=True)
     return call(
-        lambda *refs: finish_kernel(*refs, chips=chips),
+        finish_kernel,
         shape(BF16, rows, features),
         (got,),
-        scratch=[(rows, SUB, width)],
+        scratch=[tiles(rows)],
     )
 
 
 def solution(mesh):
     groups, shards = mesh.devices.shape
-    devices = mesh.devices.reshape(groups, shards // CORES, CORES)
-    fine = Mesh(devices, ("grp", "chip", "core"))
-    seq = ("chip", "core")
-    whole = ("grp", "chip", "core")
+    devices = mesh.devices.reshape(groups, -1, X_CHIPS, CORES)
+    fine = Mesh(devices, ("grp",) + CHIP + ("core",))
+    seq = CHIP + ("core",)
+    whole = ("grp",) + seq
     in_specs = (
         P(whole, None),
         P(),

time: 97.7 us -> 89 us (0.911)
  blocking collectives: 83.6 us -> 52.6 us
  waiting for transfers between devices: 3.39 us -> 14.5 us
  starting transfers between devices: 0.91 us -> 9.99 us
  Pallas kernels: 7.47 us -> 10.6 us
    all_to_all x2 -> x1, blocking collectives: 49.5 us -> 29 us  [body(): got = lax.all_to_all(sent, every, 0, 0, tiled=True)]
    all_to_all x2, blocking collectives: 34.1 us -> 23.6 us  [the longest x1 12.8 us: body(): got = lax.all_to_all(sent, ('grp', 'z'), 0, 0, tiled=True)]
    all_to_all x0 -> x1, waiting for transfers between devices: none -> 7.25 us  [body(): got = lax.all_to_all(sent, CHIP, 0, 0, tiled=True)]
    all_to_all x0 -> x1, starting transfers between devices: none -> 6.47 us  [body(): got = lax.all_to_all(sent, CHIP, 0, 0, tiled=True)]
    ppermute x1 -> x7, waiting for transfers between devices: 0.57 us -> 5.99 us  [the longest x3 5.98 us: body(): lax.ppermute(packed, 'x', [(i, (i + k) % x_chips) for i in range(x_chips)])]
    ppermute x1 -> x7, starting transfers between devices: 0.22 us -> 3.43 us  [the longest x3 2.73 us: body(): lax.ppermute(packed, 'x', [(i, (i + k) % x_chips) for i in range(x_chips)])]
    pallas_call x8 -> x7, Pallas kernels: 7.47 us -> 10.6 us  [call(): pl.pallas_call(kernel, out_shape=out_shape, in_specs=specs, out_specs=jax...]
    ppermute x2 -> x1, waiting for transfers between devices: 1.9 us -> 0.01 us  [body(): peer = lax.ppermute(got, 'core', swap)]
  transfers between devices with their start and end apart: 4 -> 10, of which waited for: 4 -> 3; matrix products, arithmetic and copies ran while one was open for 0% -> 0% of each run, Pallas kernels for 2% -> 7%
where the time goes in v3:
time: 89 us; the launch traced here: 88.7 us
  blocking collectives  52.6 us (59%)
  waiting for transfers between devices  14.5 us (16%)
  Pallas kernels  10.6 us (12%)
  starting transfers between devices  9.99 us (11%)
    all_to_all x1, blocking collectives, body(): got = lax.all_to_all(sent, every, 0, 0, tiled=True)  29 us
    all_to_all x1, blocking collectives, body(): got = lax.all_to_all(sent, ('grp', 'z'), 0, 0, tiled=True)  12.8 us
    all_to_all x1, blocking collectives, body(): got = lax.all_to_all(sent, 'z', 0, 0, tiled=True)  10.7 us
    pallas_call x7, Pallas kernels, call(): pl.pallas_call(kernel, out_shape=out_shape, in_specs=specs, out_specs=jax...  10.6 us
    all_to_all x1, waiting for transfers between devices, body(): got = lax.all_to_all(sent, CHIP, 0, 0, tiled=True)  7.25 us
    all_to_all x1, starting transfers between devices, body(): got = lax.all_to_all(sent, CHIP, 0, 0, tiled=True)  6.47 us
    ppermute x3, waiting for transfers between devices, body(): lax.ppermute(packed, 'x', [(i, (i + k) % x_chips) for i in range(x_chips)])  5.98 us
    ppermute x3, starting transfers between devices, body(): lax.ppermute(packed, 'x', [(i, (i + k) % x_chips) for i in range(x_chips)])  2.73 us
  transfers between devices with their start and end apart: 10, of which 3 were waited for; matrix products, arithmetic and copies ran while one was open for 0% of the time, Pallas kernels for 7%

profile of v3, /device:TPU:8, one launch (start us, length us, event | category | flops | bytes accessed | tf_op | source)
XLA Modules:
  0.0 88.7 jit_solution(15489648852158503026)
XLA Ops:
  0.0 1.2 %shard_map.100 = (bf16[128,8,128]{2,1,0:T(8,128)(2,1)S(1)}, bf16[192,1024]{1,0:T(8,128)(2,1)S(1)}) custom-call(bf16[4,1024]{1,0:T(4,128)(2,1)} %refs_0_.2, bf16[2,64,1024]{2,1,0:T(8,128)(2,1)} %bitcast.8, bf16[64,1024]{1,0:T(8,128)(2,1)} %refs_2_.3), custom_call_target="tpu_custom_call" | custom-call | flops 99999997952 | bytes 262144 | tf_op jit(solution)/shard_map/pallas_call | solution.py:295
  1.3 29.0 %all_to_all.26.refs_0_.refs_2_ = bf16[128,8,128]{2,1,0:T(8,128)(2,1)S(1)} all-to-all(bf16[128,8,128]{2,1,0:T(8,128)(2,1)S(1)} %get-tuple-element.11), channel_id=1, replica_groups=mesh['grp'=4,'z'=8,'x'=4,'core'=2] {'grp','z','x'}, dimensions={0} | all-to-all | bytes 524288 | tf_op jit(solution)/shard_map/all_to_all | solution.py:342
  30.3 0.0 collective-permute-start
  30.3 1.4 %collective-permute-start.4 = (bf16[192,1024]{1,0:T(8,128)(2,1)S(1)}, bf16[192,1024]{1,0:T(8,128)(2,1)S(1)}, u32[]{:S(2)}, u32[]{:S(2)}) collective-permute-start(bf16[192,1024]{1,0:T(8,128)(2,1)S(1)} %get-tuple-element.16.refs_2_), channel_id=1, source_target_pairs={{0,6},{2,0},{4,2},{6,4},{1,7},{3,1},{5,3},{7,5},{8,14},{10,8},{12,... | collective-permute-start | bytes 1179656 | tf_op jit(solution)/shard_map/ppermute | solution.py:339
  31.6 1.1 %collective-permute-start.3 = (bf16[192,1024]{1,0:T(8,128)(2,1)S(1)}, bf16[192,1024]{1,0:T(8,128)(2,1)}, u32[]{:S(2)}, u32[]{:S(2)}) collective-permute-start(bf16[192,1024]{1,0:T(8,128)(2,1)S(1)} %get-tuple-element.16.refs_2_), channel_id=1, source_target_pairs={{0,4},{2,6},{4,0},{6,2},{1,5},{3,7},{5,1},{7,3},{8,12},{10,14},{12... | collective-permute-start | bytes 1179656 | tf_op jit(solution)/shard_map/ppermute | solution.py:339
  32.7 0.3 collective-permute-start.2
  33.0 0.0 copy-start
  33.0 0.0 copy-start.5
  33.0 0.0 copy-start.6
  33.0 1.1 %shard_map.101 = (f32[8,1280]{1,0:T(8,128)S(1)}, f32[8,1024]{1,0:T(8,128)S(1)}) custom-call(bf16[128,8,128]{2,1,0:T(8,128)(2,1)S(1)} %all_to_all.26.refs_0_.refs_2_, f32[1,1024]{1,0:T(1,128)S(1)} %bitcast.5, bf16[1024,3072]{1,0:T(8,128)(2,1)S(1)} %bitcast.4), custom_call_target="tpu_custom_call" | custom-call | flops 1 | bytes 1 | tf_op jit(solution)/shard_map/pallas_call | solution.py:295
  34.2 0.0 collective-permute-done.refs_3_
  34.2 0.7 copy-done
  34.9 2.5 %shard_map.102.refs_0_ = f32[16,1280]{1,0:T(8,128)S(1)} custom-call(s32[12]{0:T(128)S(1)} %copy-done.5, s32[12]{0:T(128)S(1)} %copy-done.6, bf16[128,8,128]{2,1,0:T(8,128)(2,1)S(1)} %all_to_all.26.refs_0_.refs_2_, bf16[128,8,128]{2,1,0:T(8,128)(2,1)S(1)} %collective-permute-done.refs_3_, f32[8,1280]{1,0:T(8,128)S(1)} %get-tuple-element.12.refs_4_, ...), custom_call_target="tpu_custom_call" | custom-call | tf_op jit(solution)/shard_map/pallas_call | solution.py:295
  37.4 0.1 collective-permute-start.1
  37.5 1.3 %collective-permute-done.1.refs_1_ = f32[16,1280]{1,0:T(8,128)S(1)} collective-permute-done((f32[16,1280]{1,0:T(8,128)S(1)}, f32[16,1280]{1,0:T(8,128)S(1)}, u32[]{:S(2)}, u32[]{:S(2)}) %collective-permute-start.1) | collective-permute-done | bytes 81952 | tf_op jit(solution)/shard_map/ppermute | solution.py:360
  38.8 1.4 %shard_map.103 = bf16[32,4,1152]{2,1,0:T(4,128)(2,1)} custom-call(f32[16,1280]{1,0:T(8,128)S(1)} %shard_map.102.refs_0_, f32[16,1280]{1,0:T(8,128)S(1)} %collective-permute-done.1.refs_1_), custom_call_target="tpu_custom_call" | custom-call | tf_op jit(solution)/shard_map/pallas_call | solution.py:295
  40.2 6.5 %all-to-all-start.1 = ((bf16[32,4,1152]{2,1,0:T(4,128)(2,1)}), bf16[32,4,1152]{2,1,0:T(4,128)(2,1)S(1)}, u32[]{:S(2)}, u32[]{:S(2)}) async-start(bf16[32,4,1152]{2,1,0:T(4,128)(2,1)} %shard_map.103), calls=%async_computation.1 | async-start | bytes 589824 | tf_op jit(solution)/shard_map/all_to_all | solution.py:367
  46.7 0.1 collective-permute-start.5
  46.8 0.0 collective-permute-done.4.refs_5_
  46.8 0.5 collective-permute-start.8
  47.3 0.1 collective-permute-start.7
  47.4 6.0 %collective-permute-done.2.refs_3_ = bf16[192,1024]{1,0:T(8,128)(2,1)} collective-permute-done((bf16[192,1024]{1,0:T(8,128)(2,1)S(1)}, bf16[192,1024]{1,0:T(8,128)(2,1)}, u32[]{:S(2)}, u32[]{:S(2)}) %collective-permute-start.2) | collective-permute-done | bytes 393248 | tf_op jit(solution)/shard_map/ppermute | solution.py:339
  53.4 0.0 collective-permute-start.6
  53.4 7.2 %all-to-all-done.1.refs_0_ = bf16[32,4,1152]{2,1,0:T(4,128)(2,1)S(1)} async-done(((bf16[32,4,1152]{2,1,0:T(4,128)(2,1)}), bf16[32,4,1152]{2,1,0:T(4,128)(2,1)S(1)}, u32[]{:S(2)}, u32[]{:S(2)}) %all-to-all-start.1) | async-done | bytes 294944 | tf_op jit(solution)/shard_map/all_to_all | solution.py:367
  60.6 0.8 shard_map.104
  61.5 10.7 %all_to_all.27 = bf16[8,4,1024]{2,1,0:T(4,128)(2,1)S(1)} all-to-all(bf16[8,4,1024]{2,1,0:T(4,128)(2,1)S(1)} %all_to_all.18), channel_id=1, replica_groups=mesh['grp'=4,'z'=8,'x'=4,'core'=2] {'z'}, dimensions={0} | all-to-all | bytes 131072 | tf_op jit(solution)/shard_map/all_to_all | solution.py:374
  72.3 0.0 collective-permute-done.5.refs_6_
  72.3 0.0 collective-permute-done.7.refs_8_
  72.3 0.0 collective-permute-done.6.refs_7_
  72.3 2.9 %shard_map.105 = bf16[32,8,128]{2,1,0:T(8,128)(2,1)S(1)} custom-call(bf16[32,1024]{1,0:T(8,128)(2,1)S(1)} %all_to_all.20.refs_0_, f32[8,8,128]{2,1,0:T(8,128)S(1)} %get-tuple-element.15.refs_1_, bf16[192,1024]{1,0:T(8,128)(2,1)} %copy-done.2, bf16[192,1024]{1,0:T(8,128)(2,1)} %collective-permute-done.2.refs_3_, ...), custom_call_target="tpu_custom_call" | custom-call | tf_op jit(solution)/shard_map/pallas_call | solution.py:295
  75.2 12.8 %all_to_all.28.got = bf16[32,8,128]{2,1,0:T(8,128)(2,1)S(1)} all-to-all(bf16[32,8,128]{2,1,0:T(8,128)(2,1)S(1)} %shard_map.105), channel_id=1, replica_groups=mesh['grp'=4,'z'=8,'x'=4,'core'=2] {'grp','z'}, dimensions={0} | all-to-all | bytes 131072 | tf_op jit(solution)/shard_map/all_to_all | solution.py:387
  88.1 0.6 shard_map.106
  (21 shorter events, 0.1 us)
Async XLA Ops:
  0.0 33.0 %slice-start = ((s8[6291456]{0:T(1024)(128)(4,1)}), s8[4194304]{0:T(1024)(128)(4,1)S(1)}, s32[]{:S(2)}) async-start(s8[6291456]{0:T(1024)(128)(4,1)} %bitcast.3), calls=%async_computation.4 | async-start | bytes 8388608
  0.0 33.0 %slice-start.1 = ((s8[6291456]{0:T(1024)(128)(4,1)}), s8[2097152]{0:T(1024)(128)(4,1)S(1)}, s32[]{:S(2)}) async-start(s8[6291456]{0:T(1024)(128)(4,1)} %bitcast.3), calls=%async_computation.5 | async-start | bytes 4194304
  0.0 33.0 %copy-start.3 = (f32[1024]{0:T(1024)S(1)}, f32[1024]{0:T(1024)}, u32[]{:S(2)}) copy-start(f32[1024]{0:T(1024)} %param.11) | copy-start | bytes 12292
  1.2 45.4 %copy-start.2 = (bf16[192,1024]{1,0:T(8,128)(2,1)}, bf16[192,1024]{1,0:T(8,128)(2,1)S(1)}, u32[]{:S(2)}) copy-start(bf16[192,1024]{1,0:T(8,128)(2,1)S(1)} %get-tuple-element.16.refs_2_) | copy-start | bytes 1179652
  30.3 3.9 %collective-permute-start = (bf16[128,8,128]{2,1,0:T(8,128)(2,1)S(1)}, bf16[128,8,128]{2,1,0:T(8,128)(2,1)S(1)}, u32[]{:S(2)}, u32[]{:S(2)}) collective-permute-start(bf16[128,8,128]{2,1,0:T(8,128)(2,1)S(1)} %all_to_all.26.refs_0_.refs_2_), channel_id=1, source_target_pairs={{0,1},{1,0},{2,3},{3,2},{4,5},{5,4},{6,7},{7,6},{8,9},{9,8},{10,11... | collective-permute-start | bytes 786440 | tf_op jit(solution)/shard_map/ppermute | solution.py:343
  30.3 16.5 %collective-permute-start.4 = (bf16[192,1024]{1,0:T(8,128)(2,1)S(1)}, bf16[192,1024]{1,0:T(8,128)(2,1)S(1)}, u32[]{:S(2)}, u32[]{:S(2)}) collective-permute-start(bf16[192,1024]{1,0:T(8,128)(2,1)S(1)} %get-tuple-element.16.refs_2_), channel_id=1, source_target_pairs={{0,6},{2,0},{4,2},{6,4},{1,7},{3,1},{5,3},{7,5},{8,14},{10,8},{12,... | collective-permute-start | bytes 1179656 | tf_op jit(solution)/shard_map/ppermute | solution.py:339
  31.6 15.7 %collective-permute-start.3 = (bf16[192,1024]{1,0:T(8,128)(2,1)S(1)}, bf16[192,1024]{1,0:T(8,128)(2,1)}, u32[]{:S(2)}, u32[]{:S(2)}) collective-permute-start(bf16[192,1024]{1,0:T(8,128)(2,1)S(1)} %get-tuple-element.16.refs_2_), channel_id=1, source_target_pairs={{0,4},{2,6},{4,0},{6,2},{1,5},{3,7},{5,1},{7,3},{8,12},{10,14},{12... | collective-permute-start | bytes 1179656 | tf_op jit(solution)/shard_map/ppermute | solution.py:339
  32.7 20.7 %collective-permute-start.2 = (bf16[192,1024]{1,0:T(8,128)(2,1)S(1)}, bf16[192,1024]{1,0:T(8,128)(2,1)}, u32[]{:S(2)}, u32[]{:S(2)}) collective-permute-start(bf16[192,1024]{1,0:T(8,128)(2,1)S(1)} %get-tuple-element.16.refs_2_), channel_id=1, source_target_pairs={{0,2},{2,4},{4,6},{6,0},{1,3},{3,5},{5,7},{7,1},{8,10},{10,12},{12... | collective-permute-start | bytes 1179656 | tf_op jit(solution)/shard_map/ppermute | solution.py:339
  33.0 1.9 %copy-start = (bf16[12,2,64,1024]{3,2,1,0:T(8,128)(2,1)S(1)}, bf16[12,2,64,1024]{3,2,1,0:T(8,128)(2,1)}, u32[]{:S(2)}) copy-start(bf16[12,2,64,1024]{3,2,1,0:T(8,128)(2,1)} %refs_7_.1) | copy-start | bytes 9437188
  33.0 1.9 %copy-start.5 = (s32[12]{0:T(128)S(1)}, s32[12]{0:T(128)}, u32[]{:S(2)}) copy-start(s32[12]{0:T(128)} %refs_0_.3) | copy-start | bytes 148
  33.0 1.9 %copy-start.6 = (s32[12]{0:T(128)S(1)}, s32[12]{0:T(128)}, u32[]{:S(2)}) copy-start(s32[12]{0:T(128)} %refs_1_.1) | copy-start | bytes 148
  34.9 25.7 %copy-start.1 = (bf16[1024,1024]{1,0:T(8,128)(2,1)S(1)}, bf16[1024,1024]{1,0:T(8,128)(2,1)}, u32[]{:S(2)}) copy-start(bf16[1024,1024]{1,0:T(8,128)(2,1)} %refs_2_.5) | copy-start | bytes 6291460
  34.9 25.7 %copy-start.4 = (f32[1024]{0:T(1024)S(1)}, f32[1024]{0:T(1024)}, u32[]{:S(2)}) copy-start(f32[1024]{0:T(1024)} %param.14) | copy-start | bytes 12292
  37.4 1.4 %collective-permute-start.1 = (f32[16,1280]{1,0:T(8,128)S(1)}, f32[16,1280]{1,0:T(8,128)S(1)}, u32[]{:S(2)}, u32[]{:S(2)}) collective-permute-start(f32[16,1280]{1,0:T(8,128)S(1)} %shard_map.102.refs_0_), channel_id=1, source_target_pairs={{0,1},{1,0},{2,3},{3,2},{4,5},{5,4},{6,7},{7,6},{8,9},{9,8},{10,11... | collective-permute-start | bytes 245768 | tf_op jit(solution)/shard_map/ppermute | solution.py:360
  40.2 20.4 %all-to-all-start.1 = ((bf16[32,4,1152]{2,1,0:T(4,128)(2,1)}), bf16[32,4,1152]{2,1,0:T(4,128)(2,1)S(1)}, u32[]{:S(2)}, u32[]{:S(2)}) async-start(bf16[32,4,1152]{2,1,0:T(4,128)(2,1)} %shard_map.103), calls=%async_computation.1 | async-start | bytes 589824 | tf_op jit(solution)/shard_map/all_to_all | solution.py:367
  46.7 25.6 %collective-permute-start.5 = (bf16[192,1024]{1,0:T(8,128)(2,1)S(1)}, bf16[192,1024]{1,0:T(8,128)(2,1)}, u32[]{:S(2)}, u32[]{:S(2)}) collective-permute-start(bf16[192,1024]{1,0:T(8,128)(2,1)S(1)} %get-tuple-element.16.refs_2_), channel_id=1, source_target_pairs={{0,1},{1,0},{2,3},{3,2},{4,5},{5,4},{6,7},{7,6},{8,9},{9,8},{10,11... | collective-permute-start | bytes 1179656 | tf_op jit(solution)/shard_map/ppermute | solution.py:344
  46.8 25.5 %copy-start.7 = (bf16[192,1024]{1,0:T(8,128)(2,1)}, bf16[192,1024]{1,0:T(8,128)(2,1)S(1)}, u32[]{:S(2)}) copy-start(bf16[192,1024]{1,0:T(8,128)(2,1)S(1)} %collective-permute-done.4.refs_5_) | copy-start | bytes 1179652
  46.8 25.5 %collective-permute-start.8 = (bf16[192,1024]{1,0:T(8,128)(2,1)S(1)}, bf16[192,1024]{1,0:T(8,128)(2,1)}, u32[]{:S(2)}, u32[]{:S(2)}) collective-permute-start(bf16[192,1024]{1,0:T(8,128)(2,1)S(1)} %collective-permute-done.4.refs_5_), channel_id=1, source_target_pairs={{0,1},{1,0},{2,3},{3,2},{4,5},{5,4},{6,7},{7,6},{8,9},{9,8},{10,11... | collective-permute-start | bytes 1179656 | tf_op jit(solution)/shard_map/ppermute | solution.py:344
  47.3 25.0 %collective-permute-start.7 = (bf16[192,1024]{1,0:T(8,128)(2,1)}, bf16[192,1024]{1,0:T(8,128)(2,1)}, u32[]{:S(2)}, u32[]{:S(2)}) collective-permute-start(bf16[192,1024]{1,0:T(8,128)(2,1)} %collective-permute-done.3.refs_4_), channel_id=1, source_target_pairs={{0,1},{1,0},{2,3},{3,2},{4,5},{5,4},{6,7},{7,6},{8,9},{9,8},{10,11... | collective-permute-start | bytes 1179656 | tf_op jit(solution)/shard_map/ppermute | solution.py:344
  53.4 18.9 %collective-permute-start.6 = (bf16[192,1024]{1,0:T(8,128)(2,1)}, bf16[192,1024]{1,0:T(8,128)(2,1)}, u32[]{:S(2)}, u32[]{:S(2)}) collective-permute-start(bf16[192,1024]{1,0:T(8,128)(2,1)} %collective-permute-done.2.refs_3_), channel_id=1, source_target_pairs={{0,1},{1,0},{2,3},{3,2},{4,5},{5,4},{6,7},{7,6},{8,9},{9,8},{10,11... | collective-permute-start | bytes 1179656 | tf_op jit(solution)/shard_map/ppermute | solution.py:344

commit v4 on v3

--- a/solution.py
+++ b/solution.py
@@ -99,7 +99,7 @@
 
 
 def attend_kernel(
-    owner, fill, got, peer, own, gain, w_qkv, kv, rows_out, tiles, *, rows, chips, head_dim
+    owner, fill, got, peer, gain, w_qkv, kv, rows_out, tiles, *, rows, chips, head_dim
 ):
     blocks, _, span, features = kv.shape
     core = lax.axis_index("core")
@@ -154,10 +154,16 @@
             jnp.where(diagonal, level[part], 0.0), axis=0, keepdims=True
         )
     rows_out[:blocks, features + LANES :] = owners.astype(F32)
-    rows_out[blocks:, :] = own[SUB - rows :, :]
-
-
-def merge_kernel(mine, peer, out, flat, *, rows, head_dim):
+    spare = (rows_out.shape[0] - blocks, rows_out.shape[1])
+    rows_out[blocks:, :] = jnp.where(
+        iota(spare, 1) < features, 0.0, jnp.where(iota(spare, 1) < features + LANES, FLOOR, -1.0)
+    )
+
+
+def merge_kernel(mine_in, own, peer, out, flat, mine, *, rows, head_dim):
+    last = mine.shape[0] - rows
+    mine[...] = mine_in[...]
+    mine[last:, :] = own[SUB - rows :, :]
     count = 2 * mine.shape[0]
     features = mine.shape[1] - 2 * LANES
     half = flat.shape[0]
@@ -258,23 +264,33 @@
             first.append(pltpu.make_async_copy(weight.at[pl.ds(k * units, units)], target, sems.at[3 * n + k]))
         target = held_down.at[pl.ds(n * units, units)]
         last.append(pltpu.make_async_copy(weight.at[pl.ds(2 * units, units)], target, sems.at[3 * n + 2]))
-    for copy in first + last:
-        copy.start()
+    for k in range(2):
+        for copy in first[k * len(weights) : (k + 1) * len(weights)]:
+            copy.start()
+        for copy in last[k * len(weights) // 2 : (k + 1) * len(weights) // 2]:
+            copy.start()
     count = part.shape[0]
     line = iota((count, count), 0)
     per = count // rows
     order = (iota((count, count), 1) == (line % per) * rows + line // per).astype(BF16)
     inputs = dot(order, part[...]).astype(BF16)
-    for copy in first:
-        copy.wait()
-    both = lax.dot_general(
-        inputs, held[...], (((1,), (1,)), ((), ())), preferred_element_type=F32
-    )
-    gate = both[:, :total]
-    hidden = (gate / (1.0 + jnp.exp(-gate)) * both[:, total:]).astype(BF16)
-    for copy in last:
-        copy.wait()
-    result = dot(hidden, held_down[...])
+    result = None
+    chunk = total // 2
+    for k in range(2):
+        lo = k * chunk
+        for copy in first[k * len(weights) : (k + 1) * len(weights)]:
+            copy.wait()
+        gate, up = [
+            lax.dot_general(
+                inputs, held[at : at + chunk], (((1,), (1,)), ((), ())), preferred_element_type=F32
+            )
+            for at in (lo, total + lo)
+        ]
+        hidden = (gate / (1.0 + jnp.exp(-gate)) * up).astype(BF16)
+        for copy in last[k * len(weights) // 2 : (k + 1) * len(weights) // 2]:
+            copy.wait()
+        term = dot(hidden, held_down[lo : lo + chunk])
+        result = term if result is None else result + term
     width = result.shape[1] // SUB
     for j in range(SUB):
         tiles[:, j, :] = result[:, j * width : (j + 1) * width]
@@ -343,6 +359,15 @@
     peer = lax.ppermute(got, "core", swap)
     weights = weights + [lax.ppermute(weight, "core", swap) for weight in weights]
     gain = attn_gain.reshape(1, features)
+    partial = call(
+        lambda *refs: attend_kernel(*refs, head_dim=head_dim, **sizes),
+        shape(F32, count, features + 2 * LANES),
+        (block_owner, block_fill, got, peer, gain, w_qkv, kv_cache),
+        smem=2,
+        scratch=[tiles(blocks)],
+    )
+    got, partial = lax.optimization_barrier((got, partial))
+    partial_peer = lax.ppermute(partial, "core", swap)
     own, inputs = call(
         lambda *refs: own_kernel(*refs, head_dim=head_dim, **sizes),
         (shape(F32, SUB, features + 2 * LANES), shape(F32, SUB, features)),
@@ -350,19 +375,14 @@
         scratch=[tiles(SUB)],
         cost=pl.CostEstimate(flops=1, transcendentals=0, bytes_accessed=1),
     )
-    partial = call(
-        lambda *refs: attend_kernel(*refs, head_dim=head_dim, **sizes),
-        shape(F32, count, features + 2 * LANES),
-        (block_owner, block_fill, got, peer, own, gain, w_qkv, kv_cache),
-        smem=2,
-        scratch=[tiles(blocks)],
-    )
-    partial_peer = lax.ppermute(partial, "core", swap)
     sent = call(
         lambda *refs: merge_kernel(*refs, rows=rows, head_dim=head_dim),
         shape(BF16, chips, rows, features + LANES),
-        (partial, partial_peer),
-        scratch=[pltpu.VMEM((half, features + LANES), F32)],
+        (partial, own, partial_peer),
+        scratch=[
+            pltpu.VMEM((half, features + LANES), F32),
+            pltpu.VMEM((count, features + 2 * LANES), F32),
+        ],
     )
     got = lax.all_to_all(sent, CHIP, 0, 0, tiled=True)
     mixed, sent = call(

time: 89 us -> 87.3 us (0.981)
  waiting for transfers between devices: 14.5 us -> 13.6 us
    ppermute x3, waiting for transfers between devices: 5.98 us -> 9.3 us  [body(): lax.ppermute(packed, 'x', [(i, (i + k) % x_chips) for i in range(x_chips)])]
    all_to_all x1, waiting for transfers between devices: 7.25 us -> 4.13 us  [body(): got = lax.all_to_all(sent, CHIP, 0, 0, tiled=True)]
    ppermute x1, waiting for transfers between devices: 1.26 us -> 0.15 us  [body(): partial_peer = lax.ppermute(partial, 'core', swap)]
where the time goes in v4:
time: 87.3 us; the launch traced here: 87 us
  blocking collectives  52.7 us (60%)
  waiting for transfers between devices  13.6 us (16%)
  Pallas kernels  10.5 us (12%)
  starting transfers between devices  10 us (11%)
    all_to_all x1, blocking collectives, body(): got = lax.all_to_all(sent, every, 0, 0, tiled=True)  29 us
    all_to_all x1, blocking collectives, body(): got = lax.all_to_all(sent, ('grp', 'z'), 0, 0, tiled=True)  12.9 us
    all_to_all x1, blocking collectives, body(): got = lax.all_to_all(sent, 'z', 0, 0, tiled=True)  10.8 us
    pallas_call x7, Pallas kernels, call(): pl.pallas_call(kernel, out_shape=out_shape, in_specs=specs, out_specs=jax...  10.5 us
    ppermute x3, waiting for transfers between devices, body(): lax.ppermute(packed, 'x', [(i, (i + k) % x_chips) for i in range(x_chips)])  9.3 us
    all_to_all x1, starting transfers between devices, body(): got = lax.all_to_all(sent, CHIP, 0, 0, tiled=True)  6.48 us
    all_to_all x1, waiting for transfers between devices, body(): got = lax.all_to_all(sent, CHIP, 0, 0, tiled=True)  4.13 us
    ppermute x3, starting transfers between devices, body(): lax.ppermute(packed, 'x', [(i, (i + k) % x_chips) for i in range(x_chips)])  2.73 us
  transfers between devices with their start and end apart: 10, of which 3 were waited for; matrix products, arithmetic and copies ran while one was open for 0% of the time, Pallas kernels for 7%

profile of v4, /device:TPU:8, one launch (start us, length us, event | category | flops | bytes accessed | tf_op | source)
XLA Modules:
  0.0 87.0 jit_solution(17341782369011326541)
XLA Ops:
  0.0 1.2 %shard_map.100 = (bf16[128,8,128]{2,1,0:T(8,128)(2,1)S(1)}, bf16[192,1024]{1,0:T(8,128)(2,1)S(1)}) custom-call(bf16[4,1024]{1,0:T(4,128)(2,1)} %refs_0_.2, bf16[2,64,1024]{2,1,0:T(8,128)(2,1)} %bitcast.8, bf16[64,1024]{1,0:T(8,128)(2,1)} %refs_2_.3), custom_call_target="tpu_custom_call" | custom-call | flops 99999997952 | bytes 262144 | tf_op jit(solution)/shard_map/pallas_call | solution.py:311
  1.3 29.0 %all_to_all.26.refs_2_.refs_0_ = bf16[128,8,128]{2,1,0:T(8,128)(2,1)S(1)} all-to-all(bf16[128,8,128]{2,1,0:T(8,128)(2,1)S(1)} %get-tuple-element.13), channel_id=1, replica_groups=mesh['grp'=4,'z'=8,'x'=4,'core'=2] {'grp','z','x'}, dimensions={0} | all-to-all | bytes 524288 | tf_op jit(solution)/shard_map/all_to_all | solution.py:358
  30.3 0.0 collective-permute-start
  30.3 1.4 %collective-permute-start.4 = (bf16[192,1024]{1,0:T(8,128)(2,1)S(1)}, bf16[192,1024]{1,0:T(8,128)(2,1)S(1)}, u32[]{:S(2)}, u32[]{:S(2)}) collective-permute-start(bf16[192,1024]{1,0:T(8,128)(2,1)S(1)} %get-tuple-element.20.refs_2_), channel_id=1, source_target_pairs={{0,6},{2,0},{4,2},{6,4},{1,7},{3,1},{5,3},{7,5},{8,14},{10,8},{12,... | collective-permute-start | bytes 1179656 | tf_op jit(solution)/shard_map/ppermute | solution.py:355
  31.6 1.1 %collective-permute-start.3 = (bf16[192,1024]{1,0:T(8,128)(2,1)S(1)}, bf16[192,1024]{1,0:T(8,128)(2,1)}, u32[]{:S(2)}, u32[]{:S(2)}) collective-permute-start(bf16[192,1024]{1,0:T(8,128)(2,1)S(1)} %get-tuple-element.20.refs_2_), channel_id=1, source_target_pairs={{0,4},{2,6},{4,0},{6,2},{1,5},{3,7},{5,1},{7,3},{8,12},{10,14},{12... | collective-permute-start | bytes 1179656 | tf_op jit(solution)/shard_map/ppermute | solution.py:355
  32.7 0.3 collective-permute-start.2
  33.0 0.0 collective-permute-done.refs_3_
  33.1 2.5 %shard_map.101.refs_0_ = f32[16,1280]{1,0:T(8,128)S(1)} custom-call(s32[12]{0:T(128)S(1)} %copy-done.5, s32[12]{0:T(128)S(1)} %copy-done.6, bf16[128,8,128]{2,1,0:T(8,128)(2,1)S(1)} %all_to_all.26.refs_2_.refs_0_, bf16[128,8,128]{2,1,0:T(8,128)(2,1)S(1)} %collective-permute-done.refs_3_, f32[1,1024]{1,0:T(1,128)S(1)} %bitcast.5, ...), custom_call_target="tpu_custom_call" | custom-call | tf_op jit(solution)/shard_map/pallas_call | solution.py:311
  35.6 0.0 copy-start.1
  35.6 0.0 copy-start.4
  35.6 0.1 collective-permute-start.1
  35.7 1.1 %shard_map.102 = (f32[8,1280]{1,0:T(8,128)S(1)}, f32[8,1024]{1,0:T(8,128)S(1)}) custom-call(bf16[128,8,128]{2,1,0:T(8,128)(2,1)S(1)} %all_to_all.26.refs_2_.refs_0_, f32[1,1024]{1,0:T(1,128)S(1)} %bitcast.6, bf16[1024,3072]{1,0:T(8,128)(2,1)S(1)} %bitcast.4), custom_call_target="tpu_custom_call" | custom-call | flops 1 | bytes 1 | tf_op jit(solution)/shard_map/pallas_call | solution.py:311
  36.8 0.2 collective-permute-done.1.refs_2_
  37.0 1.4 %shard_map.103 = bf16[32,4,1152]{2,1,0:T(4,128)(2,1)} custom-call(f32[16,1280]{1,0:T(8,128)S(1)} %shard_map.101.refs_0_, f32[8,1280]{1,0:T(8,128)S(1)} %get-tuple-element.16.refs_1_, f32[16,1280]{1,0:T(8,128)S(1)} %collective-permute-done.1.refs_2_), custom_call_target="tpu_custom_call" | custom-call | tf_op jit(solution)/shard_map/pallas_call | solution.py:311
  38.4 6.5 %all-to-all-start.1 = ((bf16[32,4,1152]{2,1,0:T(4,128)(2,1)}), bf16[32,4,1152]{2,1,0:T(4,128)(2,1)S(1)}, u32[]{:S(2)}, u32[]{:S(2)}) async-start(bf16[32,4,1152]{2,1,0:T(4,128)(2,1)} %shard_map.103), calls=%async_computation.1 | async-start | bytes 589824 | tf_op jit(solution)/shard_map/all_to_all | solution.py:387
  44.9 0.2 collective-permute-start.5
  45.0 0.0 collective-permute-done.4.refs_5_
  45.0 0.4 collective-permute-start.8
  45.5 0.0 collective-permute-done.3.refs_4_
  45.5 0.1 collective-permute-start.7
  45.6 9.3 %collective-permute-done.2.refs_3_ = bf16[192,1024]{1,0:T(8,128)(2,1)} collective-permute-done((bf16[192,1024]{1,0:T(8,128)(2,1)S(1)}, bf16[192,1024]{1,0:T(8,128)(2,1)}, u32[]{:S(2)}, u32[]{:S(2)}) %collective-permute-start.2) | collective-permute-done | bytes 393248 | tf_op jit(solution)/shard_map/ppermute | solution.py:355
  54.9 0.0 collective-permute-start.6
  54.9 4.1 %all-to-all-done.1.refs_0_ = bf16[32,4,1152]{2,1,0:T(4,128)(2,1)S(1)} async-done(((bf16[32,4,1152]{2,1,0:T(4,128)(2,1)}), bf16[32,4,1152]{2,1,0:T(4,128)(2,1)S(1)}, u32[]{:S(2)}, u32[]{:S(2)}) %all-to-all-start.1) | async-done | bytes 294944 | tf_op jit(solution)/shard_map/all_to_all | solution.py:387
  59.1 0.8 shard_map.104
  59.9 10.8 %all_to_all.27 = bf16[8,4,1024]{2,1,0:T(4,128)(2,1)S(1)} all-to-all(bf16[8,4,1024]{2,1,0:T(4,128)(2,1)S(1)} %all_to_all.18), channel_id=1, replica_groups=mesh['grp'=4,'z'=8,'x'=4,'core'=2] {'z'}, dimensions={0} | all-to-all | bytes 131072 | tf_op jit(solution)/shard_map/all_to_all | solution.py:394
  70.7 0.0 collective-permute-done.5.refs_6_
  70.7 0.0 collective-permute-done.8.refs_9_
  70.7 0.0 collective-permute-done.7.refs_8_
  70.7 0.0 collective-permute-done.6.refs_7_
  70.7 2.8 %shard_map.105 = bf16[32,8,128]{2,1,0:T(8,128)(2,1)S(1)} custom-call(bf16[32,1024]{1,0:T(8,128)(2,1)S(1)} %all_to_all.20.refs_0_, f32[8,8,128]{2,1,0:T(8,128)S(1)} %get-tuple-element.19.refs_1_, bf16[192,1024]{1,0:T(8,128)(2,1)} %copy-done.2, bf16[192,1024]{1,0:T(8,128)(2,1)} %collective-permute-done.2.refs_3_, ...), custom_call_target="tpu_custom_call" | custom-call | tf_op jit(solution)/shard_map/pallas_call | solution.py:311
  73.5 12.9 %all_to_all.28.got = bf16[32,8,128]{2,1,0:T(8,128)(2,1)S(1)} all-to-all(bf16[32,8,128]{2,1,0:T(8,128)(2,1)S(1)} %shard_map.105), channel_id=1, replica_groups=mesh['grp'=4,'z'=8,'x'=4,'core'=2] {'grp','z'}, dimensions={0} | all-to-all | bytes 131072 | tf_op jit(solution)/shard_map/all_to_all | solution.py:407
  86.4 0.6 shard_map.106
  (21 shorter events, 0.1 us)
Async XLA Ops:
  0.0 33.0 %slice-start = ((s8[6291456]{0:T(1024)(128)(4,1)}), s8[4194304]{0:T(1024)(128)(4,1)S(1)}, s32[]{:S(2)}) async-start(s8[6291456]{0:T(1024)(128)(4,1)} %bitcast.3), calls=%async_computation.4 | async-start | bytes 8388608
  0.0 33.0 %slice-start.1 = ((s8[6291456]{0:T(1024)(128)(4,1)}), s8[2097152]{0:T(1024)(128)(4,1)S(1)}, s32[]{:S(2)}) async-start(s8[6291456]{0:T(1024)(128)(4,1)} %bitcast.3), calls=%async_computation.5 | async-start | bytes 4194304
  0.0 33.0 %copy-start = (bf16[12,2,64,1024]{3,2,1,0:T(8,128)(2,1)S(1)}, bf16[12,2,64,1024]{3,2,1,0:T(8,128)(2,1)}, u32[]{:S(2)}) copy-start(bf16[12,2,64,1024]{3,2,1,0:T(8,128)(2,1)} %refs_6_.1) | copy-start | bytes 9437188
  0.0 33.0 %copy-start.3 = (f32[1024]{0:T(1024)S(1)}, f32[1024]{0:T(1024)}, u32[]{:S(2)}) copy-start(f32[1024]{0:T(1024)} %param.11) | copy-start | bytes 12292
  0.0 33.0 %copy-start.5 = (s32[12]{0:T(128)S(1)}, s32[12]{0:T(128)}, u32[]{:S(2)}) copy-start(s32[12]{0:T(128)} %refs_0_.3) | copy-start | bytes 148
  0.0 33.0 %copy-start.6 = (s32[12]{0:T(128)S(1)}, s32[12]{0:T(128)}, u32[]{:S(2)}) copy-start(s32[12]{0:T(128)} %refs_1_.1) | copy-start | bytes 148
  1.3 43.6 %copy-start.2 = (bf16[192,1024]{1,0:T(8,128)(2,1)}, bf16[192,1024]{1,0:T(8,128)(2,1)S(1)}, u32[]{:S(2)}) copy-start(bf16[192,1024]{1,0:T(8,128)(2,1)S(1)} %get-tuple-element.20.refs_2_) | copy-start | bytes 1179652
  30.3 2.7 %collective-permute-start = (bf16[128,8,128]{2,1,0:T(8,128)(2,1)S(1)}, bf16[128,8,128]{2,1,0:T(8,128)(2,1)S(1)}, u32[]{:S(2)}, u32[]{:S(2)}) collective-permute-start(bf16[128,8,128]{2,1,0:T(8,128)(2,1)S(1)} %all_to_all.26.refs_2_.refs_0_), channel_id=1, source_target_pairs={{0,1},{1,0},{2,3},{3,2},{4,5},{5,4},{6,7},{7,6},{8,9},{9,8},{10,11... | collective-permute-start | bytes 786440 | tf_op jit(solution)/shard_map/ppermute | solution.py:359
  30.3 14.8 %collective-permute-start.4 = (bf16[192,1024]{1,0:T(8,128)(2,1)S(1)}, bf16[192,1024]{1,0:T(8,128)(2,1)S(1)}, u32[]{:S(2)}, u32[]{:S(2)}) collective-permute-start(bf16[192,1024]{1,0:T(8,128)(2,1)S(1)} %get-tuple-element.20.refs_2_), channel_id=1, source_target_pairs={{0,6},{2,0},{4,2},{6,4},{1,7},{3,1},{5,3},{7,5},{8,14},{10,8},{12,... | collective-permute-start | bytes 1179656 | tf_op jit(solution)/shard_map/ppermute | solution.py:355
  31.6 13.9 %collective-permute-start.3 = (bf16[192,1024]{1,0:T(8,128)(2,1)S(1)}, bf16[192,1024]{1,0:T(8,128)(2,1)}, u32[]{:S(2)}, u32[]{:S(2)}) collective-permute-start(bf16[192,1024]{1,0:T(8,128)(2,1)S(1)} %get-tuple-element.20.refs_2_), channel_id=1, source_target_pairs={{0,4},{2,6},{4,0},{6,2},{1,5},{3,7},{5,1},{7,3},{8,12},{10,14},{12... | collective-permute-start | bytes 1179656 | tf_op jit(solution)/shard_map/ppermute | solution.py:355
  32.7 22.2 %collective-permute-start.2 = (bf16[192,1024]{1,0:T(8,128)(2,1)S(1)}, bf16[192,1024]{1,0:T(8,128)(2,1)}, u32[]{:S(2)}, u32[]{:S(2)}) collective-permute-start(bf16[192,1024]{1,0:T(8,128)(2,1)S(1)} %get-tuple-element.20.refs_2_), channel_id=1, source_target_pairs={{0,2},{2,4},{4,6},{6,0},{1,3},{3,5},{5,7},{7,1},{8,10},{10,12},{12... | collective-permute-start | bytes 1179656 | tf_op jit(solution)/shard_map/ppermute | solution.py:355
  35.6 23.5 %copy-start.1 = (bf16[1024,1024]{1,0:T(8,128)(2,1)S(1)}, bf16[1024,1024]{1,0:T(8,128)(2,1)}, u32[]{:S(2)}) copy-start(bf16[1024,1024]{1,0:T(8,128)(2,1)} %refs_2_.5) | copy-start | bytes 6291460
  35.6 23.5 %copy-start.4 = (f32[1024]{0:T(1024)S(1)}, f32[1024]{0:T(1024)}, u32[]{:S(2)}) copy-start(f32[1024]{0:T(1024)} %param.14) | copy-start | bytes 12292
  35.6 1.4 %collective-permute-start.1 = (f32[16,1280]{1,0:T(8,128)S(1)}, f32[16,1280]{1,0:T(8,128)S(1)}, u32[]{:S(2)}, u32[]{:S(2)}) collective-permute-start(f32[16,1280]{1,0:T(8,128)S(1)} %shard_map.101.refs_0_), channel_id=1, source_target_pairs={{0,1},{1,0},{2,3},{3,2},{4,5},{5,4},{6,7},{7,6},{8,9},{9,8},{10,11... | collective-permute-start | bytes 245768 | tf_op jit(solution)/shard_map/ppermute | solution.py:370
  38.4 20.6 %all-to-all-start.1 = ((bf16[32,4,1152]{2,1,0:T(4,128)(2,1)}), bf16[32,4,1152]{2,1,0:T(4,128)(2,1)S(1)}, u32[]{:S(2)}, u32[]{:S(2)}) async-start(bf16[32,4,1152]{2,1,0:T(4,128)(2,1)} %shard_map.103), calls=%async_computation.1 | async-start | bytes 589824 | tf_op jit(solution)/shard_map/all_to_all | solution.py:387
  44.9 25.8 %collective-permute-start.5 = (bf16[192,1024]{1,0:T(8,128)(2,1)S(1)}, bf16[192,1024]{1,0:T(8,128)(2,1)}, u32[]{:S(2)}, u32[]{:S(2)}) collective-permute-start(bf16[192,1024]{1,0:T(8,128)(2,1)S(1)} %get-tuple-element.20.refs_2_), channel_id=1, source_target_pairs={{0,1},{1,0},{2,3},{3,2},{4,5},{5,4},{6,7},{7,6},{8,9},{9,8},{10,11... | collective-permute-start | bytes 1179656 | tf_op jit(solution)/shard_map/ppermute | solution.py:360
  45.0 25.7 %copy-start.7 = (bf16[192,1024]{1,0:T(8,128)(2,1)}, bf16[192,1024]{1,0:T(8,128)(2,1)S(1)}, u32[]{:S(2)}) copy-start(bf16[192,1024]{1,0:T(8,128)(2,1)S(1)} %collective-permute-done.4.refs_5_) | copy-start | bytes 1179652
  45.0 25.7 %collective-permute-start.8 = (bf16[192,1024]{1,0:T(8,128)(2,1)S(1)}, bf16[192,1024]{1,0:T(8,128)(2,1)}, u32[]{:S(2)}, u32[]{:S(2)}) collective-permute-start(bf16[192,1024]{1,0:T(8,128)(2,1)S(1)} %collective-permute-done.4.refs_5_), channel_id=1, source_target_pairs={{0,1},{1,0},{2,3},{3,2},{4,5},{5,4},{6,7},{7,6},{8,9},{9,8},{10,11... | collective-permute-start | bytes 1179656 | tf_op jit(solution)/shard_map/ppermute | solution.py:360
  45.5 25.2 %collective-permute-start.7 = (bf16[192,1024]{1,0:T(8,128)(2,1)}, bf16[192,1024]{1,0:T(8,128)(2,1)}, u32[]{:S(2)}, u32[]{:S(2)}) collective-permute-start(bf16[192,1024]{1,0:T(8,128)(2,1)} %collective-permute-done.3.refs_4_), channel_id=1, source_target_pairs={{0,1},{1,0},{2,3},{3,2},{4,5},{5,4},{6,7},{7,6},{8,9},{9,8},{10,11... | collective-permute-start | bytes 1179656 | tf_op jit(solution)/shard_map/ppermute | solution.py:360
  54.9 15.8 %collective-permute-start.6 = (bf16[192,1024]{1,0:T(8,128)(2,1)}, bf16[192,1024]{1,0:T(8,128)(2,1)}, u32[]{:S(2)}, u32[]{:S(2)}) collective-permute-start(bf16[192,1024]{1,0:T(8,128)(2,1)} %collective-permute-done.2.refs_3_), channel_id=1, source_target_pairs={{0,1},{1,0},{2,3},{3,2},{4,5},{5,4},{6,7},{7,6},{8,9},{9,8},{10,11... | collective-permute-start | bytes 1179656 | tf_op jit(solution)/shard_map/ppermute | solution.py:360

commit v5 on v4

--- a/solution.py
+++ b/solution.py
@@ -115,43 +115,30 @@
     query = dot(rms_scaled(inputs, gain[...]), w_qkv[:, :features]).astype(BF16).astype(F32)
 
     head_mask = iota((HEADS, features), 1) // head_dim == iota((HEADS, features), 0)
-    spread = jnp.concatenate(
-        [
-            jnp.where(head_mask, jnp.broadcast_to(query[b : b + 1], (HEADS, features)), 0.0)
-            for b in range(blocks)
-        ],
-        axis=0,
-    ).astype(BF16)
-    keys = kv[:, 0].reshape(blocks * span, features)
-    values = kv[:, 1].reshape(blocks * span, features)
-    scores = lax.dot_general(
-        spread, keys, (((1,), (1,)), ((), ())), preferred_element_type=F32
-    ) * (head_dim**-0.5)
-    wide = scores.shape
-    column = iota(wide, 1)
-    column_block = column // span
-    limit = jnp.zeros((1, blocks * span), jnp.int32)
-    limit_block = iota(limit.shape, 1) // span
+    diagonal = iota((HEADS, LANES), 0) == iota((HEADS, LANES), 1)
+    nt = (((1,), (1,)), ((), ()))
+    scores = []
     for b in range(blocks):
-        limit = jnp.where(limit_block == b, fill[b], limit)
-    live = (column_block == iota(wide, 0) // HEADS) & (column - column_block * span < limit)
-    masked = jnp.where(live, scores, FLOOR)
-    peak = jnp.max(masked, axis=1, keepdims=True)
-    weights = jnp.where(live, jnp.exp(masked - peak), 0.0).astype(BF16)
-    total = jnp.sum(weights.astype(F32), axis=1, keepdims=True)
-    summed = dot(weights, values)
-    alive = total > 0.0
-    safe = jnp.where(alive, total, 1.0)
-    level = jnp.where(alive, peak + jnp.log(safe), FLOOR)
-    summed = summed * (1.0 / safe)
-    diagonal = iota((HEADS, LANES), 0) == iota((HEADS, LANES), 1)
+        row = jnp.broadcast_to(query[b : b + 1], (HEADS, features))
+        spread = jnp.where(head_mask, row, 0.0).astype(BF16)
+        scores.append(lax.dot_general(spread, kv[b, 0], nt, preferred_element_type=F32))
+    column = iota((HEADS, span), 1)
     for b in range(blocks):
-        part = slice(b * HEADS, (b + 1) * HEADS)
+        live = column < fill[b]
+        masked = jnp.where(live, scores[b] * (head_dim**-0.5), FLOOR)
+        peak = jnp.max(masked, axis=1, keepdims=True)
+        weights = jnp.where(live, jnp.exp(masked - peak), 0.0).astype(BF16)
+        total = jnp.sum(weights.astype(F32), axis=1, keepdims=True)
+        summed = dot(weights, kv[b, 1])
+        alive = total > 0.0
+        safe = jnp.where(alive, total, 1.0)
+        level = jnp.where(alive, peak + jnp.log(safe), FLOOR)
+        summed = summed * (1.0 / safe)
         rows_out[b : b + 1, :features] = jnp.sum(
-            jnp.where(head_mask, summed[part], 0.0), axis=0, keepdims=True
+            jnp.where(head_mask, summed, 0.0), axis=0, keepdims=True
         )
         rows_out[b : b + 1, features : features + LANES] = jnp.sum(
-            jnp.where(diagonal, level[part], 0.0), axis=0, keepdims=True
+            jnp.where(diagonal, level, 0.0), axis=0, keepdims=True
         )
     rows_out[:blocks, features + LANES :] = owners.astype(F32)
     spare = (rows_out.shape[0] - blocks, rows_out.shape[1])

time: 87.3 us -> 86.8 us (level)
    ppermute x3, waiting for transfers between devices: 9.3 us -> 10.4 us  [body(): lax.ppermute(packed, 'x', [(i, (i + k) % x_chips) for i in range(x_chips)])]
    all_to_all x1, waiting for transfers between devices: 4.13 us -> 3.15 us  [body(): got = lax.all_to_all(sent, CHIP, 0, 0, tiled=True)]
  transfers between devices with their start and end apart: 10 -> 10, of which waited for: 3 -> 4; matrix products, arithmetic and copies ran while one was open for 0% -> 0% of each run, Pallas kernels for 7% -> 6%
where the time goes in v5:
time: 86.8 us; the launch traced here: 86.5 us
  blocking collectives  52.7 us (61%)
  waiting for transfers between devices  13.7 us (16%)
  Pallas kernels  9.96 us (11%)
  starting transfers between devices  9.91 us (11%)
    all_to_all x1, blocking collectives, body(): got = lax.all_to_all(sent, every, 0, 0, tiled=True)  29 us
    all_to_all x1, blocking collectives, body(): got = lax.all_to_all(sent, ('grp', 'z'), 0, 0, tiled=True)  12.9 us
    all_to_all x1, blocking collectives, body(): got = lax.all_to_all(sent, 'z', 0, 0, tiled=True)  10.8 us
    ppermute x3, waiting for transfers between devices, body(): lax.ppermute(packed, 'x', [(i, (i + k) % x_chips) for i in range(x_chips)])  10.4 us
    pallas_call x7, Pallas kernels, call(): pl.pallas_call(kernel, out_shape=out_shape, in_specs=specs, out_specs=jax...  9.96 us
    all_to_all x1, starting transfers between devices, body(): got = lax.all_to_all(sent, CHIP, 0, 0, tiled=True)  6.48 us
    all_to_all x1, waiting for transfers between devices, body(): got = lax.all_to_all(sent, CHIP, 0, 0, tiled=True)  3.15 us
    ppermute x3, starting transfers between devices, body(): lax.ppermute(packed, 'x', [(i, (i + k) % x_chips) for i in range(x_chips)])  2.73 us
  transfers between devices with their start and end apart: 10, of which 4 were waited for; matrix products, arithmetic and copies ran while one was open for 0% of the time, Pallas kernels for 6%

profile of v5, /device:TPU:8, one launch (start us, length us, event | category | flops | bytes accessed | tf_op | source)
XLA Modules:
  0.0 86.5 jit_solution(12692195872196834110)
XLA Ops:
  0.0 1.2 %shard_map.100 = (bf16[128,8,128]{2,1,0:T(8,128)(2,1)S(1)}, bf16[192,1024]{1,0:T(8,128)(2,1)S(1)}) custom-call(bf16[4,1024]{1,0:T(4,128)(2,1)} %refs_0_.2, bf16[2,64,1024]{2,1,0:T(8,128)(2,1)} %bitcast.8, bf16[64,1024]{1,0:T(8,128)(2,1)} %refs_2_.3), custom_call_target="tpu_custom_call" | custom-call | flops 99999997952 | bytes 262144 | tf_op jit(solution)/shard_map/pallas_call | solution.py:298
  1.3 29.0 %all_to_all.26.refs_2_.refs_0_ = bf16[128,8,128]{2,1,0:T(8,128)(2,1)S(1)} all-to-all(bf16[128,8,128]{2,1,0:T(8,128)(2,1)S(1)} %get-tuple-element.13), channel_id=1, replica_groups=mesh['grp'=4,'z'=8,'x'=4,'core'=2] {'grp','z','x'}, dimensions={0} | all-to-all | bytes 524288 | tf_op jit(solution)/shard_map/all_to_all | solution.py:345
  30.3 0.0 collective-permute-start
  30.3 1.4 %collective-permute-start.4 = (bf16[192,1024]{1,0:T(8,128)(2,1)S(1)}, bf16[192,1024]{1,0:T(8,128)(2,1)S(1)}, u32[]{:S(2)}, u32[]{:S(2)}) collective-permute-start(bf16[192,1024]{1,0:T(8,128)(2,1)S(1)} %get-tuple-element.20.refs_2_), channel_id=1, source_target_pairs={{0,6},{2,0},{4,2},{6,4},{1,7},{3,1},{5,3},{7,5},{8,14},{10,8},{12,... | collective-permute-start | bytes 1179656 | tf_op jit(solution)/shard_map/ppermute | solution.py:342
  31.6 1.1 %collective-permute-start.3 = (bf16[192,1024]{1,0:T(8,128)(2,1)S(1)}, bf16[192,1024]{1,0:T(8,128)(2,1)}, u32[]{:S(2)}, u32[]{:S(2)}) collective-permute-start(bf16[192,1024]{1,0:T(8,128)(2,1)S(1)} %get-tuple-element.20.refs_2_), channel_id=1, source_target_pairs={{0,4},{2,6},{4,0},{6,2},{1,5},{3,7},{5,1},{7,3},{8,12},{10,14},{12... | collective-permute-start | bytes 1179656 | tf_op jit(solution)/shard_map/ppermute | solution.py:342
  32.7 0.3 collective-permute-start.2
  33.0 0.0 collective-permute-done.refs_3_
  33.1 2.0 %shard_map.101.refs_0_ = f32[16,1280]{1,0:T(8,128)S(1)} custom-call(s32[12]{0:T(128)S(1)} %copy-done.5, s32[12]{0:T(128)S(1)} %copy-done.6, bf16[128,8,128]{2,1,0:T(8,128)(2,1)S(1)} %all_to_all.26.refs_2_.refs_0_, bf16[128,8,128]{2,1,0:T(8,128)(2,1)S(1)} %collective-permute-done.refs_3_, f32[1,1024]{1,0:T(1,128)S(1)} %bitcast.5, ...), custom_call_target="tpu_custom_call" | custom-call | tf_op jit(solution)/shard_map/pallas_call | solution.py:298
  35.1 0.0 copy-start.1
  35.1 0.0 copy-start.4
  35.1 0.1 collective-permute-start.1
  35.2 1.1 %shard_map.102 = (f32[8,1280]{1,0:T(8,128)S(1)}, f32[8,1024]{1,0:T(8,128)S(1)}) custom-call(bf16[128,8,128]{2,1,0:T(8,128)(2,1)S(1)} %all_to_all.26.refs_2_.refs_0_, f32[1,1024]{1,0:T(1,128)S(1)} %bitcast.6, bf16[1024,3072]{1,0:T(8,128)(2,1)S(1)} %bitcast.4), custom_call_target="tpu_custom_call" | custom-call | flops 1 | bytes 1 | tf_op jit(solution)/shard_map/pallas_call | solution.py:298
  36.3 0.2 collective-permute-done.1.refs_2_
  36.4 1.4 %shard_map.103 = bf16[32,4,1152]{2,1,0:T(4,128)(2,1)} custom-call(f32[16,1280]{1,0:T(8,128)S(1)} %shard_map.101.refs_0_, f32[8,1280]{1,0:T(8,128)S(1)} %get-tuple-element.16.refs_1_, f32[16,1280]{1,0:T(8,128)S(1)} %collective-permute-done.1.refs_2_), custom_call_target="tpu_custom_call" | custom-call | tf_op jit(solution)/shard_map/pallas_call | solution.py:298
  37.9 6.5 %all-to-all-start.1 = ((bf16[32,4,1152]{2,1,0:T(4,128)(2,1)}), bf16[32,4,1152]{2,1,0:T(4,128)(2,1)S(1)}, u32[]{:S(2)}, u32[]{:S(2)}) async-start(bf16[32,4,1152]{2,1,0:T(4,128)(2,1)} %shard_map.103), calls=%async_computation.1 | async-start | bytes 589824 | tf_op jit(solution)/shard_map/all_to_all | solution.py:374
  44.4 0.2 collective-permute-start.5
  44.5 0.0 collective-permute-done.4.refs_5_
  44.5 0.4 collective-permute-start.8
  45.0 0.3 collective-permute-done.3.refs_4_
  45.2 0.0 collective-permute-start.7
  45.2 10.1 %collective-permute-done.2.refs_3_ = bf16[192,1024]{1,0:T(8,128)(2,1)} collective-permute-done((bf16[192,1024]{1,0:T(8,128)(2,1)S(1)}, bf16[192,1024]{1,0:T(8,128)(2,1)}, u32[]{:S(2)}, u32[]{:S(2)}) %collective-permute-start.2) | collective-permute-done | bytes 393248 | tf_op jit(solution)/shard_map/ppermute | solution.py:342
  55.4 0.0 collective-permute-start.6
  55.4 3.1 %all-to-all-done.1.refs_0_ = bf16[32,4,1152]{2,1,0:T(4,128)(2,1)S(1)} async-done(((bf16[32,4,1152]{2,1,0:T(4,128)(2,1)}), bf16[32,4,1152]{2,1,0:T(4,128)(2,1)S(1)}, u32[]{:S(2)}, u32[]{:S(2)}) %all-to-all-start.1) | async-done | bytes 294944 | tf_op jit(solution)/shard_map/all_to_all | solution.py:374
  58.5 0.8 shard_map.104
  59.4 10.8 %all_to_all.27 = bf16[8,4,1024]{2,1,0:T(4,128)(2,1)S(1)} all-to-all(bf16[8,4,1024]{2,1,0:T(4,128)(2,1)S(1)} %all_to_all.18), channel_id=1, replica_groups=mesh['grp'=4,'z'=8,'x'=4,'core'=2] {'z'}, dimensions={0} | all-to-all | bytes 131072 | tf_op jit(solution)/shard_map/all_to_all | solution.py:381
  70.2 0.0 collective-permute-done.5.refs_6_
  70.2 0.0 collective-permute-done.8.refs_9_
  70.2 0.0 collective-permute-done.7.refs_8_
  70.2 0.0 collective-permute-done.6.refs_7_
  70.2 2.8 %shard_map.105 = bf16[32,8,128]{2,1,0:T(8,128)(2,1)S(1)} custom-call(bf16[32,1024]{1,0:T(8,128)(2,1)S(1)} %all_to_all.20.refs_0_, f32[8,8,128]{2,1,0:T(8,128)S(1)} %get-tuple-element.19.refs_1_, bf16[192,1024]{1,0:T(8,128)(2,1)} %copy-done.2, bf16[192,1024]{1,0:T(8,128)(2,1)} %collective-permute-done.2.refs_3_, ...), custom_call_target="tpu_custom_call" | custom-call | tf_op jit(solution)/shard_map/pallas_call | solution.py:298
  73.0 12.9 %all_to_all.28.got = bf16[32,8,128]{2,1,0:T(8,128)(2,1)S(1)} all-to-all(bf16[32,8,128]{2,1,0:T(8,128)(2,1)S(1)} %shard_map.105), channel_id=1, replica_groups=mesh['grp'=4,'z'=8,'x'=4,'core'=2] {'grp','z'}, dimensions={0} | all-to-all | bytes 131072 | tf_op jit(solution)/shard_map/all_to_all | solution.py:394
  85.9 0.6 shard_map.106
  (21 shorter events, 0.1 us)
Async XLA Ops:
  0.0 33.0 %slice-start = ((s8[6291456]{0:T(1024)(128)(4,1)}), s8[4194304]{0:T(1024)(128)(4,1)S(1)}, s32[]{:S(2)}) async-start(s8[6291456]{0:T(1024)(128)(4,1)} %bitcast.3), calls=%async_computation.4 | async-start | bytes 8388608
  0.0 33.0 %slice-start.1 = ((s8[6291456]{0:T(1024)(128)(4,1)}), s8[2097152]{0:T(1024)(128)(4,1)S(1)}, s32[]{:S(2)}) async-start(s8[6291456]{0:T(1024)(128)(4,1)} %bitcast.3), calls=%async_computation.5 | async-start | bytes 4194304
  0.0 33.0 %copy-start = (bf16[12,2,64,1024]{3,2,1,0:T(8,128)(2,1)S(1)}, bf16[12,2,64,1024]{3,2,1,0:T(8,128)(2,1)}, u32[]{:S(2)}) copy-start(bf16[12,2,64,1024]{3,2,1,0:T(8,128)(2,1)} %refs_6_.1) | copy-start | bytes 9437188
  0.0 33.0 %copy-start.3 = (f32[1024]{0:T(1024)S(1)}, f32[1024]{0:T(1024)}, u32[]{:S(2)}) copy-start(f32[1024]{0:T(1024)} %param.11) | copy-start | bytes 12292
  0.0 33.0 %copy-start.5 = (s32[12]{0:T(128)S(1)}, s32[12]{0:T(128)}, u32[]{:S(2)}) copy-start(s32[12]{0:T(128)} %refs_0_.3) | copy-start | bytes 148
  0.0 33.0 %copy-start.6 = (s32[12]{0:T(128)S(1)}, s32[12]{0:T(128)}, u32[]{:S(2)}) copy-start(s32[12]{0:T(128)} %refs_1_.1) | copy-start | bytes 148
  1.3 43.1 %copy-start.2 = (bf16[192,1024]{1,0:T(8,128)(2,1)}, bf16[192,1024]{1,0:T(8,128)(2,1)S(1)}, u32[]{:S(2)}) copy-start(bf16[192,1024]{1,0:T(8,128)(2,1)S(1)} %get-tuple-element.20.refs_2_) | copy-start | bytes 1179652
  30.3 2.7 %collective-permute-start = (bf16[128,8,128]{2,1,0:T(8,128)(2,1)S(1)}, bf16[128,8,128]{2,1,0:T(8,128)(2,1)S(1)}, u32[]{:S(2)}, u32[]{:S(2)}) collective-permute-start(bf16[128,8,128]{2,1,0:T(8,128)(2,1)S(1)} %all_to_all.26.refs_2_.refs_0_), channel_id=1, source_target_pairs={{0,1},{1,0},{2,3},{3,2},{4,5},{5,4},{6,7},{7,6},{8,9},{9,8},{10,11... | collective-permute-start | bytes 786440 | tf_op jit(solution)/shard_map/ppermute | solution.py:346
  30.3 14.2 %collective-permute-start.4 = (bf16[192,1024]{1,0:T(8,128)(2,1)S(1)}, bf16[192,1024]{1,0:T(8,128)(2,1)S(1)}, u32[]{:S(2)}, u32[]{:S(2)}) collective-permute-start(bf16[192,1024]{1,0:T(8,128)(2,1)S(1)} %get-tuple-element.20.refs_2_), channel_id=1, source_target_pairs={{0,6},{2,0},{4,2},{6,4},{1,7},{3,1},{5,3},{7,5},{8,14},{10,8},{12,... | collective-permute-start | bytes 1179656 | tf_op jit(solution)/shard_map/ppermute | solution.py:342
  31.6 13.6 %collective-permute-start.3 = (bf16[192,1024]{1,0:T(8,128)(2,1)S(1)}, bf16[192,1024]{1,0:T(8,128)(2,1)}, u32[]{:S(2)}, u32[]{:S(2)}) collective-permute-start(bf16[192,1024]{1,0:T(8,128)(2,1)S(1)} %get-tuple-element.20.refs_2_), channel_id=1, source_target_pairs={{0,4},{2,6},{4,0},{6,2},{1,5},{3,7},{5,1},{7,3},{8,12},{10,14},{12... | collective-permute-start | bytes 1179656 | tf_op jit(solution)/shard_map/ppermute | solution.py:342
  32.7 22.7 %collective-permute-start.2 = (bf16[192,1024]{1,0:T(8,128)(2,1)S(1)}, bf16[192,1024]{1,0:T(8,128)(2,1)}, u32[]{:S(2)}, u32[]{:S(2)}) collective-permute-start(bf16[192,1024]{1,0:T(8,128)(2,1)S(1)} %get-tuple-element.20.refs_2_), channel_id=1, source_target_pairs={{0,2},{2,4},{4,6},{6,0},{1,3},{3,5},{5,7},{7,1},{8,10},{10,12},{12... | collective-permute-start | bytes 1179656 | tf_op jit(solution)/shard_map/ppermute | solution.py:342
  35.1 23.5 %copy-start.1 = (bf16[1024,1024]{1,0:T(8,128)(2,1)S(1)}, bf16[1024,1024]{1,0:T(8,128)(2,1)}, u32[]{:S(2)}) copy-start(bf16[1024,1024]{1,0:T(8,128)(2,1)} %refs_2_.5) | copy-start | bytes 6291460
  35.1 23.5 %copy-start.4 = (f32[1024]{0:T(1024)S(1)}, f32[1024]{0:T(1024)}, u32[]{:S(2)}) copy-start(f32[1024]{0:T(1024)} %param.14) | copy-start | bytes 12292
  35.1 1.4 %collective-permute-start.1 = (f32[16,1280]{1,0:T(8,128)S(1)}, f32[16,1280]{1,0:T(8,128)S(1)}, u32[]{:S(2)}, u32[]{:S(2)}) collective-permute-start(f32[16,1280]{1,0:T(8,128)S(1)} %shard_map.101.refs_0_), channel_id=1, source_target_pairs={{0,1},{1,0},{2,3},{3,2},{4,5},{5,4},{6,7},{7,6},{8,9},{9,8},{10,11... | collective-permute-start | bytes 245768 | tf_op jit(solution)/shard_map/ppermute | solution.py:357
  37.9 20.7 %all-to-all-start.1 = ((bf16[32,4,1152]{2,1,0:T(4,128)(2,1)}), bf16[32,4,1152]{2,1,0:T(4,128)(2,1)S(1)}, u32[]{:S(2)}, u32[]{:S(2)}) async-start(bf16[32,4,1152]{2,1,0:T(4,128)(2,1)} %shard_map.103), calls=%async_computation.1 | async-start | bytes 589824 | tf_op jit(solution)/shard_map/all_to_all | solution.py:374
  44.4 25.8 %collective-permute-start.5 = (bf16[192,1024]{1,0:T(8,128)(2,1)S(1)}, bf16[192,1024]{1,0:T(8,128)(2,1)}, u32[]{:S(2)}, u32[]{:S(2)}) collective-permute-start(bf16[192,1024]{1,0:T(8,128)(2,1)S(1)} %get-tuple-element.20.refs_2_), channel_id=1, source_target_pairs={{0,1},{1,0},{2,3},{3,2},{4,5},{5,4},{6,7},{7,6},{8,9},{9,8},{10,11... | collective-permute-start | bytes 1179656 | tf_op jit(solution)/shard_map/ppermute | solution.py:347
  44.5 25.7 %copy-start.7 = (bf16[192,1024]{1,0:T(8,128)(2,1)}, bf16[192,1024]{1,0:T(8,128)(2,1)S(1)}, u32[]{:S(2)}) copy-start(bf16[192,1024]{1,0:T(8,128)(2,1)S(1)} %collective-permute-done.4.refs_5_) | copy-start | bytes 1179652
  44.5 25.7 %collective-permute-start.8 = (bf16[192,1024]{1,0:T(8,128)(2,1)S(1)}, bf16[192,1024]{1,0:T(8,128)(2,1)}, u32[]{:S(2)}, u32[]{:S(2)}) collective-permute-start(bf16[192,1024]{1,0:T(8,128)(2,1)S(1)} %collective-permute-done.4.refs_5_), channel_id=1, source_target_pairs={{0,1},{1,0},{2,3},{3,2},{4,5},{5,4},{6,7},{7,6},{8,9},{9,8},{10,11... | collective-permute-start | bytes 1179656 | tf_op jit(solution)/shard_map/ppermute | solution.py:347
  45.2 25.0 %collective-permute-start.7 = (bf16[192,1024]{1,0:T(8,128)(2,1)}, bf16[192,1024]{1,0:T(8,128)(2,1)}, u32[]{:S(2)}, u32[]{:S(2)}) collective-permute-start(bf16[192,1024]{1,0:T(8,128)(2,1)} %collective-permute-done.3.refs_4_), channel_id=1, source_target_pairs={{0,1},{1,0},{2,3},{3,2},{4,5},{5,4},{6,7},{7,6},{8,9},{9,8},{10,11... | collective-permute-start | bytes 1179656 | tf_op jit(solution)/shard_map/ppermute | solution.py:347
  55.4 14.8 %collective-permute-start.6 = (bf16[192,1024]{1,0:T(8,128)(2,1)}, bf16[192,1024]{1,0:T(8,128)(2,1)}, u32[]{:S(2)}, u32[]{:S(2)}) collective-permute-start(bf16[192,1024]{1,0:T(8,128)(2,1)} %collective-permute-done.2.refs_3_), channel_id=1, source_target_pairs={{0,1},{1,0},{2,3},{3,2},{4,5},{5,4},{6,7},{7,6},{8,9},{9,8},{10,11... | collective-permute-start | bytes 1179656 | tf_op jit(solution)/shard_map/ppermute | solution.py:347

commit v6 on v5

--- a/solution.py
+++ b/solution.py
@@ -205,8 +205,11 @@
     stats = dot(first_table, packed)
     absent = jnp.sum(table.astype(F32), axis=1, keepdims=True) == 0.0
     flat[:, features:] = jnp.where(absent & (iota(stats.shape, 1) < HEADS), FLOOR, stats)
-    for n in range(out.shape[0]):
-        out[n] = flat[n * rows : (n + 1) * rows, :].astype(BF16)
+    step = 2 * rows
+    for n in range(out.shape[0] // 2):
+        pair = flat[n * step : (n + 1) * step, :].astype(BF16)
+        out[2 * n] = pair[:rows]
+        out[2 * n + 1] = pair[rows:]
 
 
 def project_kernel(parts_in, inputs, w_out, gain, mixed_out, sent, got, *, rows, head_dim):
@@ -257,10 +260,8 @@
         for copy in last[k * len(weights) // 2 : (k + 1) * len(weights) // 2]:
             copy.start()
     count = part.shape[0]
-    line = iota((count, count), 0)
     per = count // rows
-    order = (iota((count, count), 1) == (line % per) * rows + line // per).astype(BF16)
-    inputs = dot(order, part[...]).astype(BF16)
+    inputs = part[...]
     result = None
     chunk = total // 2
     for k in range(2):
@@ -283,8 +284,10 @@
         tiles[:, j, :] = result[:, j * width : (j + 1) * width]
     z = lax.axis_index("z")
     for i in range(rows):
-        tiles[i * per + z] = tiles[i * per + z] + mixed[i]
-    out[...] = tiles[...].astype(BF16)
+        tiles[z * rows + i] = tiles[z * rows + i] + mixed[i]
+    for i in range(rows):
+        for n in range(per):
+            out[i * per + n] = tiles[n * rows + i].astype(BF16)
 
 
 def call(kernel, out_shape, args, smem=0, hbm=(), out_specs=None, scratch=(), limit=12 << 20, cost=None):

time: 86.8 us -> 86.8 us (level)
  no operation moved by 1% of the time
where the time goes in v6:
time: 86.8 us; the launch traced here: 86.5 us
  blocking collectives  52.6 us (61%)
  waiting for transfers between devices  13.7 us (16%)
  Pallas kernels  9.92 us (11%)
  starting transfers between devices  9.91 us (11%)
    all_to_all x1, blocking collectives, body(): got = lax.all_to_all(sent, every, 0, 0, tiled=True)  29 us
    all_to_all x1, blocking collectives, body(): got = lax.all_to_all(sent, ('grp', 'z'), 0, 0, tiled=True)  12.9 us
    all_to_all x1, blocking collectives, body(): got = lax.all_to_all(sent, 'z', 0, 0, tiled=True)  10.8 us
    ppermute x3, waiting for transfers between devices, body(): lax.ppermute(packed, 'x', [(i, (i + k) % x_chips) for i in range(x_chips)])  10.5 us
    pallas_call x7, Pallas kernels, call(): pl.pallas_call(kernel, out_shape=out_shape, in_specs=specs, out_specs=jax...  9.92 us
    all_to_all x1, starting transfers between devices, body(): got = lax.all_to_all(sent, CHIP, 0, 0, tiled=True)  6.48 us
    all_to_all x1, waiting for transfers between devices, body(): got = lax.all_to_all(sent, CHIP, 0, 0, tiled=True)  3.08 us
    ppermute x3, starting transfers between devices, body(): lax.ppermute(packed, 'x', [(i, (i + k) % x_chips) for i in range(x_chips)])  2.73 us
  transfers between devices with their start and end apart: 10, of which 4 were waited for; matrix products, arithmetic and copies ran while one was open for 0% of the time, Pallas kernels for 6%

profile of v6, /device:TPU:8, one launch (start us, length us, event | category | flops | bytes accessed | tf_op | source)
XLA Modules:
  0.0 86.5 jit_solution(16312402199090648928)
XLA Ops:
  0.0 1.2 %shard_map.100 = (bf16[128,8,128]{2,1,0:T(8,128)(2,1)S(1)}, bf16[192,1024]{1,0:T(8,128)(2,1)S(1)}) custom-call(bf16[4,1024]{1,0:T(4,128)(2,1)} %refs_0_.2, bf16[2,64,1024]{2,1,0:T(8,128)(2,1)} %bitcast.8, bf16[64,1024]{1,0:T(8,128)(2,1)} %refs_2_.3), custom_call_target="tpu_custom_call" | custom-call | flops 99999997952 | bytes 262144 | tf_op jit(solution)/shard_map/pallas_call | solution.py:301
  1.3 29.0 %all_to_all.26.refs_2_.refs_0_ = bf16[128,8,128]{2,1,0:T(8,128)(2,1)S(1)} all-to-all(bf16[128,8,128]{2,1,0:T(8,128)(2,1)S(1)} %get-tuple-element.13), channel_id=1, replica_groups=mesh['grp'=4,'z'=8,'x'=4,'core'=2] {'grp','z','x'}, dimensions={0} | all-to-all | bytes 524288 | tf_op jit(solution)/shard_map/all_to_all | solution.py:348
  30.3 0.0 collective-permute-start
  30.3 1.4 %collective-permute-start.4 = (bf16[192,1024]{1,0:T(8,128)(2,1)S(1)}, bf16[192,1024]{1,0:T(8,128)(2,1)S(1)}, u32[]{:S(2)}, u32[]{:S(2)}) collective-permute-start(bf16[192,1024]{1,0:T(8,128)(2,1)S(1)} %get-tuple-element.20.refs_2_), channel_id=1, source_target_pairs={{0,6},{2,0},{4,2},{6,4},{1,7},{3,1},{5,3},{7,5},{8,14},{10,8},{12,... | collective-permute-start | bytes 1179656 | tf_op jit(solution)/shard_map/ppermute | solution.py:345
  31.6 1.1 %collective-permute-start.3 = (bf16[192,1024]{1,0:T(8,128)(2,1)S(1)}, bf16[192,1024]{1,0:T(8,128)(2,1)}, u32[]{:S(2)}, u32[]{:S(2)}) collective-permute-start(bf16[192,1024]{1,0:T(8,128)(2,1)S(1)} %get-tuple-element.20.refs_2_), channel_id=1, source_target_pairs={{0,4},{2,6},{4,0},{6,2},{1,5},{3,7},{5,1},{7,3},{8,12},{10,14},{12... | collective-permute-start | bytes 1179656 | tf_op jit(solution)/shard_map/ppermute | solution.py:345
  32.7 0.3 collective-permute-start.2
  33.0 0.0 collective-permute-done.refs_3_
  33.1 2.0 %shard_map.101.refs_0_ = f32[16,1280]{1,0:T(8,128)S(1)} custom-call(s32[12]{0:T(128)S(1)} %copy-done.5, s32[12]{0:T(128)S(1)} %copy-done.6, bf16[128,8,128]{2,1,0:T(8,128)(2,1)S(1)} %all_to_all.26.refs_2_.refs_0_, bf16[128,8,128]{2,1,0:T(8,128)(2,1)S(1)} %collective-permute-done.refs_3_, f32[1,1024]{1,0:T(1,128)S(1)} %bitcast.5, ...), custom_call_target="tpu_custom_call" | custom-call | tf_op jit(solution)/shard_map/pallas_call | solution.py:301
  35.1 0.0 copy-start.1
  35.1 0.0 copy-start.4
  35.1 0.1 collective-permute-start.1
  35.2 1.1 %shard_map.102 = (f32[8,1280]{1,0:T(8,128)S(1)}, f32[8,1024]{1,0:T(8,128)S(1)}) custom-call(bf16[128,8,128]{2,1,0:T(8,128)(2,1)S(1)} %all_to_all.26.refs_2_.refs_0_, f32[1,1024]{1,0:T(1,128)S(1)} %bitcast.6, bf16[1024,3072]{1,0:T(8,128)(2,1)S(1)} %bitcast.4), custom_call_target="tpu_custom_call" | custom-call | flops 1 | bytes 1 | tf_op jit(solution)/shard_map/pallas_call | solution.py:301
  36.3 0.2 collective-permute-done.1.refs_2_
  36.4 1.4 %shard_map.103 = bf16[32,4,1152]{2,1,0:T(4,128)(2,1)} custom-call(f32[16,1280]{1,0:T(8,128)S(1)} %shard_map.101.refs_0_, f32[8,1280]{1,0:T(8,128)S(1)} %get-tuple-element.16.refs_1_, f32[16,1280]{1,0:T(8,128)S(1)} %collective-permute-done.1.refs_2_), custom_call_target="tpu_custom_call" | custom-call | tf_op jit(solution)/shard_map/pallas_call | solution.py:301
  37.8 6.5 %all-to-all-start.1 = ((bf16[32,4,1152]{2,1,0:T(4,128)(2,1)}), bf16[32,4,1152]{2,1,0:T(4,128)(2,1)S(1)}, u32[]{:S(2)}, u32[]{:S(2)}) async-start(bf16[32,4,1152]{2,1,0:T(4,128)(2,1)} %shard_map.103), calls=%async_computation.1 | async-start | bytes 589824 | tf_op jit(solution)/shard_map/all_to_all | solution.py:377
  44.3 0.2 collective-permute-start.5
  44.5 0.0 collective-permute-done.4.refs_5_
  44.5 0.4 collective-permute-start.8
  44.9 0.3 collective-permute-done.3.refs_4_
  45.2 0.0 collective-permute-start.7
  45.2 10.2 %collective-permute-done.2.refs_3_ = bf16[192,1024]{1,0:T(8,128)(2,1)} collective-permute-done((bf16[192,1024]{1,0:T(8,128)(2,1)S(1)}, bf16[192,1024]{1,0:T(8,128)(2,1)}, u32[]{:S(2)}, u32[]{:S(2)}) %collective-permute-start.2) | collective-permute-done | bytes 393248 | tf_op jit(solution)/shard_map/ppermute | solution.py:345
  55.4 0.0 collective-permute-start.6
  55.4 3.1 %all-to-all-done.1.refs_0_ = bf16[32,4,1152]{2,1,0:T(4,128)(2,1)S(1)} async-done(((bf16[32,4,1152]{2,1,0:T(4,128)(2,1)}), bf16[32,4,1152]{2,1,0:T(4,128)(2,1)S(1)}, u32[]{:S(2)}, u32[]{:S(2)}) %all-to-all-start.1) | async-done | bytes 294944 | tf_op jit(solution)/shard_map/all_to_all | solution.py:377
  58.5 0.8 shard_map.104
  59.4 10.8 %all_to_all.27 = bf16[8,4,1024]{2,1,0:T(4,128)(2,1)S(1)} all-to-all(bf16[8,4,1024]{2,1,0:T(4,128)(2,1)S(1)} %all_to_all.18), channel_id=1, replica_groups=mesh['grp'=4,'z'=8,'x'=4,'core'=2] {'z'}, dimensions={0} | all-to-all | bytes 131072 | tf_op jit(solution)/shard_map/all_to_all | solution.py:384
  70.1 0.0 collective-permute-done.5.refs_6_
  70.2 0.0 collective-permute-done.8.refs_9_
  70.2 0.0 collective-permute-done.7.refs_8_
  70.2 0.0 collective-permute-done.6.refs_7_
  70.2 2.8 %shard_map.105 = bf16[32,8,128]{2,1,0:T(8,128)(2,1)S(1)} custom-call(bf16[32,1024]{1,0:T(8,128)(2,1)S(1)} %all_to_all.20.refs_0_, f32[8,8,128]{2,1,0:T(8,128)S(1)} %get-tuple-element.19.refs_1_, bf16[192,1024]{1,0:T(8,128)(2,1)} %copy-done.2, bf16[192,1024]{1,0:T(8,128)(2,1)} %collective-permute-done.2.refs_3_, ...), custom_call_target="tpu_custom_call" | custom-call | tf_op jit(solution)/shard_map/pallas_call | solution.py:301
  73.0 12.9 %all_to_all.28.got = bf16[32,8,128]{2,1,0:T(8,128)(2,1)S(1)} all-to-all(bf16[32,8,128]{2,1,0:T(8,128)(2,1)S(1)} %shard_map.105), channel_id=1, replica_groups=mesh['grp'=4,'z'=8,'x'=4,'core'=2] {'grp','z'}, dimensions={0} | all-to-all | bytes 131072 | tf_op jit(solution)/shard_map/all_to_all | solution.py:397
  85.9 0.6 shard_map.106
  (21 shorter events, 0.1 us)
Async XLA Ops:
  0.0 33.0 %slice-start = ((s8[6291456]{0:T(1024)(128)(4,1)}), s8[4194304]{0:T(1024)(128)(4,1)S(1)}, s32[]{:S(2)}) async-start(s8[6291456]{0:T(1024)(128)(4,1)} %bitcast.3), calls=%async_computation.4 | async-start | bytes 8388608
  0.0 33.0 %slice-start.1 = ((s8[6291456]{0:T(1024)(128)(4,1)}), s8[2097152]{0:T(1024)(128)(4,1)S(1)}, s32[]{:S(2)}) async-start(s8[6291456]{0:T(1024)(128)(4,1)} %bitcast.3), calls=%async_computation.5 | async-start | bytes 4194304
  0.0 33.0 %copy-start = (bf16[12,2,64,1024]{3,2,1,0:T(8,128)(2,1)S(1)}, bf16[12,2,64,1024]{3,2,1,0:T(8,128)(2,1)}, u32[]{:S(2)}) copy-start(bf16[12,2,64,1024]{3,2,1,0:T(8,128)(2,1)} %refs_6_.1) | copy-start | bytes 9437188
  0.0 33.0 %copy-start.3 = (f32[1024]{0:T(1024)S(1)}, f32[1024]{0:T(1024)}, u32[]{:S(2)}) copy-start(f32[1024]{0:T(1024)} %param.11) | copy-start | bytes 12292
  0.0 33.0 %copy-start.5 = (s32[12]{0:T(128)S(1)}, s32[12]{0:T(128)}, u32[]{:S(2)}) copy-start(s32[12]{0:T(128)} %refs_0_.3) | copy-start | bytes 148
  0.0 33.0 %copy-start.6 = (s32[12]{0:T(128)S(1)}, s32[12]{0:T(128)}, u32[]{:S(2)}) copy-start(s32[12]{0:T(128)} %refs_1_.1) | copy-start | bytes 148
  1.3 43.1 %copy-start.2 = (bf16[192,1024]{1,0:T(8,128)(2,1)}, bf16[192,1024]{1,0:T(8,128)(2,1)S(1)}, u32[]{:S(2)}) copy-start(bf16[192,1024]{1,0:T(8,128)(2,1)S(1)} %get-tuple-element.20.refs_2_) | copy-start | bytes 1179652
  30.3 2.7 %collective-permute-start = (bf16[128,8,128]{2,1,0:T(8,128)(2,1)S(1)}, bf16[128,8,128]{2,1,0:T(8,128)(2,1)S(1)}, u32[]{:S(2)}, u32[]{:S(2)}) collective-permute-start(bf16[128,8,128]{2,1,0:T(8,128)(2,1)S(1)} %all_to_all.26.refs_2_.refs_0_), channel_id=1, source_target_pairs={{0,1},{1,0},{2,3},{3,2},{4,5},{5,4},{6,7},{7,6},{8,9},{9,8},{10,11... | collective-permute-start | bytes 786440 | tf_op jit(solution)/shard_map/ppermute | solution.py:349
  30.3 14.2 %collective-permute-start.4 = (bf16[192,1024]{1,0:T(8,128)(2,1)S(1)}, bf16[192,1024]{1,0:T(8,128)(2,1)S(1)}, u32[]{:S(2)}, u32[]{:S(2)}) collective-permute-start(bf16[192,1024]{1,0:T(8,128)(2,1)S(1)} %get-tuple-element.20.refs_2_), channel_id=1, source_target_pairs={{0,6},{2,0},{4,2},{6,4},{1,7},{3,1},{5,3},{7,5},{8,14},{10,8},{12,... | collective-permute-start | bytes 1179656 | tf_op jit(solution)/shard_map/ppermute | solution.py:345
  31.6 13.6 %collective-permute-start.3 = (bf16[192,1024]{1,0:T(8,128)(2,1)S(1)}, bf16[192,1024]{1,0:T(8,128)(2,1)}, u32[]{:S(2)}, u32[]{:S(2)}) collective-permute-start(bf16[192,1024]{1,0:T(8,128)(2,1)S(1)} %get-tuple-element.20.refs_2_), channel_id=1, source_target_pairs={{0,4},{2,6},{4,0},{6,2},{1,5},{3,7},{5,1},{7,3},{8,12},{10,14},{12... | collective-permute-start | bytes 1179656 | tf_op jit(solution)/shard_map/ppermute | solution.py:345
  32.7 22.7 %collective-permute-start.2 = (bf16[192,1024]{1,0:T(8,128)(2,1)S(1)}, bf16[192,1024]{1,0:T(8,128)(2,1)}, u32[]{:S(2)}, u32[]{:S(2)}) collective-permute-start(bf16[192,1024]{1,0:T(8,128)(2,1)S(1)} %get-tuple-element.20.refs_2_), channel_id=1, source_target_pairs={{0,2},{2,4},{4,6},{6,0},{1,3},{3,5},{5,7},{7,1},{8,10},{10,12},{12... | collective-permute-start | bytes 1179656 | tf_op jit(solution)/shard_map/ppermute | solution.py:345
  35.1 23.4 %copy-start.1 = (bf16[1024,1024]{1,0:T(8,128)(2,1)S(1)}, bf16[1024,1024]{1,0:T(8,128)(2,1)}, u32[]{:S(2)}) copy-start(bf16[1024,1024]{1,0:T(8,128)(2,1)} %refs_2_.5) | copy-start | bytes 6291460
  35.1 23.4 %copy-start.4 = (f32[1024]{0:T(1024)S(1)}, f32[1024]{0:T(1024)}, u32[]{:S(2)}) copy-start(f32[1024]{0:T(1024)} %param.14) | copy-start | bytes 12292
  35.1 1.4 %collective-permute-start.1 = (f32[16,1280]{1,0:T(8,128)S(1)}, f32[16,1280]{1,0:T(8,128)S(1)}, u32[]{:S(2)}, u32[]{:S(2)}) collective-permute-start(f32[16,1280]{1,0:T(8,128)S(1)} %shard_map.101.refs_0_), channel_id=1, source_target_pairs={{0,1},{1,0},{2,3},{3,2},{4,5},{5,4},{6,7},{7,6},{8,9},{9,8},{10,11... | collective-permute-start | bytes 245768 | tf_op jit(solution)/shard_map/ppermute | solution.py:360
  37.8 20.6 %all-to-all-start.1 = ((bf16[32,4,1152]{2,1,0:T(4,128)(2,1)}), bf16[32,4,1152]{2,1,0:T(4,128)(2,1)S(1)}, u32[]{:S(2)}, u32[]{:S(2)}) async-start(bf16[32,4,1152]{2,1,0:T(4,128)(2,1)} %shard_map.103), calls=%async_computation.1 | async-start | bytes 589824 | tf_op jit(solution)/shard_map/all_to_all | solution.py:377
  44.3 25.8 %collective-permute-start.5 = (bf16[192,1024]{1,0:T(8,128)(2,1)S(1)}, bf16[192,1024]{1,0:T(8,128)(2,1)}, u32[]{:S(2)}, u32[]{:S(2)}) collective-permute-start(bf16[192,1024]{1,0:T(8,128)(2,1)S(1)} %get-tuple-element.20.refs_2_), channel_id=1, source_target_pairs={{0,1},{1,0},{2,3},{3,2},{4,5},{5,4},{6,7},{7,6},{8,9},{9,8},{10,11... | collective-permute-start | bytes 1179656 | tf_op jit(solution)/shard_map/ppermute | solution.py:350
  44.5 25.7 %copy-start.7 = (bf16[192,1024]{1,0:T(8,128)(2,1)}, bf16[192,1024]{1,0:T(8,128)(2,1)S(1)}, u32[]{:S(2)}) copy-start(bf16[192,1024]{1,0:T(8,128)(2,1)S(1)} %collective-permute-done.4.refs_5_) | copy-start | bytes 1179652
  44.5 25.7 %collective-permute-start.8 = (bf16[192,1024]{1,0:T(8,128)(2,1)S(1)}, bf16[192,1024]{1,0:T(8,128)(2,1)}, u32[]{:S(2)}, u32[]{:S(2)}) collective-permute-start(bf16[192,1024]{1,0:T(8,128)(2,1)S(1)} %collective-permute-done.4.refs_5_), channel_id=1, source_target_pairs={{0,1},{1,0},{2,3},{3,2},{4,5},{5,4},{6,7},{7,6},{8,9},{9,8},{10,11... | collective-permute-start | bytes 1179656 | tf_op jit(solution)/shard_map/ppermute | solution.py:350
  45.2 24.9 %collective-permute-start.7 = (bf16[192,1024]{1,0:T(8,128)(2,1)}, bf16[192,1024]{1,0:T(8,128)(2,1)}, u32[]{:S(2)}, u32[]{:S(2)}) collective-permute-start(bf16[192,1024]{1,0:T(8,128)(2,1)} %collective-permute-done.3.refs_4_), channel_id=1, source_target_pairs={{0,1},{1,0},{2,3},{3,2},{4,5},{5,4},{6,7},{7,6},{8,9},{9,8},{10,11... | collective-permute-start | bytes 1179656 | tf_op jit(solution)/shard_map/ppermute | solution.py:350
  55.4 14.8 %collective-permute-start.6 = (bf16[192,1024]{1,0:T(8,128)(2,1)}, bf16[192,1024]{1,0:T(8,128)(2,1)}, u32[]{:S(2)}, u32[]{:S(2)}) collective-permute-start(bf16[192,1024]{1,0:T(8,128)(2,1)} %collective-permute-done.2.refs_3_), channel_id=1, source_target_pairs={{0,1},{1,0},{2,3},{3,2},{4,5},{5,4},{6,7},{7,6},{8,9},{9,8},{10,11... | collective-permute-start | bytes 1179656 | tf_op jit(solution)/shard_map/ppermute | solution.py:350
